TPU v7x, 32 devices: a whole 2x2x4 slice. The times are simulated.
32 devices in a mesh: rep: 4 (over z), shard: 8 (over y, x, core).
Axes of the slice: x: 2, y: 2, z: 4, core: 2. Of those that a mesh axis runs over, the one named last changes fastest.
Arguments:
- tokens: bfloat16 [16384, 1024], P(('rep', 'shard')), may hold values from -6 to 6
- cotangent: bfloat16 [16384, 1024], P(('rep', 'shard')), may hold values from -6 to 6
- seq_lengths: int32 [32, 4], P(('rep', 'shard')), may hold values from 1 to 256, 512 in all within a row
- pack_order: int32 [16384], P(('rep', 'shard')), may hold values from 0 to 511, as said below
- unpack_order: int32 [16384], P(('rep', 'shard')), may hold values from 0 to 511, as said below
- expert_ids: int32 [16384, 8], P(('rep', 'shard')), may hold values from 0 to 15, all different within a row; in each aligned block of 512 rows (0 to 511, 512 to 1023, ...) at most 384 rows name the same one
- gates: float32 [16384, 8], P(('rep', 'shard')), may hold values from 0.06 to 0.19
- first_gain: bfloat16 [1024], P('shard'), may hold values from 0.5 to 1.5
- query_weight: bfloat16 [1024, 1024], P('shard'), may hold values from -0.1875 to 0.1875
- key_matrix: bfloat16 [1024, 512], P('shard'), may hold values from -0.1875 to 0.1875
- value_matrix: bfloat16 [1024, 512], P('shard'), may hold values from -0.1875 to 0.1875
- output_weight: bfloat16 [1024, 1024], P('shard'), may hold values from -0.75 to 0.75
- second_gain: bfloat16 [1024], P('shard'), may hold values from 0.5 to 1.5
- gate_weight: bfloat16 [16, 1024, 512], P('shard'), may hold values from -0.1875 to 0.1875
- up_weight: bfloat16 [16, 1024, 512], P('shard'), may hold values from -0.1875 to 0.1875
- down_weight: bfloat16 [16, 512, 1024], P('shard'), may hold values from -1 to 1
Outputs:
- out_tokens: bfloat16 [16384, 1024], P(('rep', 'shard'))
- delta_tokens: bfloat16 [16384, 1024], P(('rep', 'shard'))
- delta_first: float32 [1024], P('shard')
- delta_query: float32 [1024, 1024], P('shard')
- delta_key: float32 [1024, 512], P('shard')
- delta_value: float32 [1024, 512], P('shard')
- delta_output: float32 [1024, 1024], P('shard')
- delta_second: float32 [1024], P('shard')
- delta_gate: float32 [16, 1024, 512], P('shard')
- delta_up: float32 [16, 1024, 512], P('shard')
- delta_down: float32 [16, 512, 1024], P('shard')
Inputs may be any that keep to these rules, and one draw needn't show every extreme that they name: `seq_lengths`: each row sums to 512, and its longest entry is exactly 256. `pack_order`: the 512 entries of each pack form a permutation. `unpack_order`: the 512 entries of each pack form the inverse of that pack's permutation in pack_order. `expert_ids`: A row names 8 different experts; among the 512 rows of one pack no expert is named more than 384 times, and in some pack one expert is named exactly 384 times.
All inputs are finite; a program needn't handle non-finite values.
Results may differ from a plain program's by a relative error of at most 0.02.
Values may be sent and summed in bfloat16 or wider, within the bound.
A program may use at most 256 MiB of HBM per device.

v0:
```python
import functools

import jax
import jax.numpy as jnp
import numpy as np
from jax import lax
from jax.experimental import pallas as pl
from jax.experimental.pallas import tpu as pltpu
from jax.sharding import PartitionSpec as P

QUERY_HEADS = 16
KEY_VALUE_HEADS = 8
HEAD_SIZE = 64


EPS = 1e-05
THETA = 10000.0


MESH = pl.DeviceIdType.MESH
NN = (((1,), (0,)), ((), ()))
NT = (((1,), (1,)), ((), ()))
TN = (((0,), (0,)), ((), ()))
TILE = 256
VMEM_MOST = 66_000_000


def matmul(left, right, dims):
    return lax.dot_general(left, right, dims, preferred_element_type=jnp.float32)


def stage_in(refs, count, start=0):
    held = refs[-count - 1 : -1]
    copies = [
        pltpu.make_async_copy(refs[start + k], held[k], refs[-1].at[k]) for k in range(count)
    ]
    return held, copies, refs[: -count - 1]


def flip(number, mask, count):
    out = 0
    bit = 1
    while bit < count:
        a = (number // bit) % 2
        b = (mask // bit) % 2
        out = out + (a + b - 2 * a * b) * bit
        bit *= 2
    return out


def greet(me, rep, count, reps=1):
    barrier = pltpu.get_barrier_semaphore()
    for k in range(1, count):
        pl.semaphore_signal(
            barrier, inc=1, device_id=(rep, lax.rem(me + k, count)), device_id_type=MESH
        )
    for k in range(1, reps):
        pl.semaphore_signal(
            barrier, inc=1, device_id=(lax.rem(rep + k, reps), me), device_id_type=MESH
        )
    pl.semaphore_wait(barrier, count + reps - 2)


LINE = 4
LAG = 2
RING = 4


class Line:
    def __init__(
        self,
        rep,
        me,
        source,
        out,
        first,
        second,
        both,
        sends,
        recvs,
        held=None,
        sems=None,
        base=0,
        count=None,
    ):
        self.rep, self.me = rep, me
        self.source, self.out = source, out
        self.first, self.second, self.both = first, second, both
        self.sends, self.recvs = sends, recvs
        self.held, self.sems = held, sems
        self.base = base
        self.count = source.shape[0] if count is None else count
        self.outer = (rep == 0) | (rep == LINE - 1)
        self.inner = jnp.logical_not(self.outer)
        self.inside = jnp.where(rep == 0, 1, 2)
        self.outside = jnp.where(rep == 1, 0, 3)
        self.across = LINE - 1 - rep

    def copy(self, stage, i):
        ring = self.both.at[i % RING]
        if stage == 0:
            source = self.source.at[self.base + i]
        else:
            source = ring if stage == 1 else self.first.at[i]
        target = (self.first, self.second, self.first)[stage].at[i]
        device = (self.inside, self.across, self.outside)[stage]
        return pltpu.make_async_remote_copy(
            src_ref=source,
            dst_ref=target,
            send_sem=self.sends.at[stage, i],
            recv_sem=self.recvs.at[stage, i],
            device_id=(device, self.me),
            device_id_type=MESH,
        )

    def load(self, i):
        return pltpu.make_async_copy(
            self.source.at[self.base + i], self.held.at[i % 2], self.sems.at[self.count + i % 2]
        )

    def put(self, i):
        return pltpu.make_async_copy(self.first.at[i], self.out.at[i], self.sems.at[i])

    def loop(self, body, begin=0):
        def step(i, carry):
            body(i)
            return carry

        lax.fori_loop(begin, self.count, step, 0)

    def start(self, begin=0, end=None):
        end = self.count if end is None else end

        @pl.when(self.outer)
        def _():
            def step(i, carry):
                self.copy(0, i).start()
                return carry

            lax.fori_loop(begin, end, step, 0)

        if self.held is not None:

            @pl.when(self.inner)
            def _():
                self.load(0).start()

    def tick(self, j):
        full = jnp.float32
        low = jnp.bfloat16

        @pl.when(self.inner & (j >= 0) & (j < self.count))
        def _():
            if self.held is None:
                own = self.source[self.base + j]
            else:

                @pl.when(j + 1 < self.count)
                def _():
                    self.load(j + 1).start()

                self.load(j).wait()
                own = self.held[j % 2]
            self.copy(0, j).wait_recv()

            @pl.when(j >= RING)
            def _():
                self.copy(1, j - RING).wait_send()

            self.both[j % RING] = (own.astype(full) + self.first[j].astype(full)).astype(low)
            self.copy(1, j).start()

        i = j - LAG

        @pl.when(self.inner & (i >= 0) & (i < self.count))
        def _():
            self.copy(1, i).wait_recv()
            every = self.both[i % RING].astype(full) + self.second[i].astype(full)
            self.first[i] = every.astype(low)
            self.copy(2, i).start()
            if self.held is None:
                self.out[i] = every.astype(low)
            else:
                self.put(i).start()

    def ticks(self, begin, end):
        def step(j, carry):
            self.tick(j)
            return carry

        lax.fori_loop(begin, end, step, 0)

    def finish(self):
        @pl.when(self.outer)
        def _():
            def receive(i):
                self.copy(2, i).wait_recv()
                if self.held is None:
                    self.out[i] = self.first[i]
                else:
                    self.put(i).start()

            self.loop(receive)
            self.loop(lambda i: self.copy(0, i).wait_send())

        @pl.when(self.inner)
        def _():
            self.loop(lambda i: self.copy(1, i).wait_send(), self.count - RING)
            self.loop(lambda i: self.copy(2, i).wait_send())

        if self.held is not None:
            self.loop(lambda i: self.put(i).wait())


def line_scratch(shape, streamed=True):
    low = jnp.bfloat16
    dma = pltpu.SemaphoreType.DMA
    scratch = [
        pltpu.VMEM(shape, low),
        pltpu.VMEM(shape, low),
        pltpu.VMEM((RING,) + shape[1:], low),
        dma((3, shape[0])),
        dma((3, shape[0])),
    ]
    if streamed:
        scratch += [pltpu.VMEM((2,) + shape[1:], low), dma((shape[0] + 2,))]
    return scratch


def remote(source, target, sends, recvs, index, device):
    return pltpu.make_async_remote_copy(
        src_ref=source,
        dst_ref=target,
        send_sem=sends.at[index],
        recv_sem=recvs.at[index],
        device_id=device,
        device_id_type=MESH,
    )


class Gather:
    def __init__(self, count, rep, me, own, slot, sends, recvs):
        self.count, self.rep, self.me = count, rep, me
        self.own, self.slot, self.sends, self.recvs = own, slot, sends, recvs
        self.waiting = []

    def near(self, mask):
        return flip(self.me, mask, self.count)

    def send(self, source, owner, part, mask, index):
        remote(
            source,
            self.slot(owner, part),
            self.sends,
            self.recvs,
            index,
            (self.rep, self.near(mask)),
        ).start()
        self.waiting.append(index)

    def arrived(self, owner, part, index):
        remote(
            self.slot(owner, part),
            self.slot(owner, part),
            self.sends,
            self.recvs,
            index,
            (self.rep, self.me),
        ).wait_recv()

    def pass_on(self, mask, part, index, new, onward):
        owner = self.near(mask)
        if index is not None:
            self.arrived(owner, part, index)
        self.send(self.slot(owner, part), owner, part, onward, new)

    def start(self):
        if self.count == 8:
            plan = ((2, 0, 0), (4, 1, 1), (2, 1, 2), (4, 0, 3), (1, 0, 4), (1, 1, 5))
            for mask, part, index in plan:
                self.send(self.own(part), self.me, part, mask, index)
        else:
            for mask in [1] + list(range(2, self.count, 2)):
                for part in range(2):
                    self.send(self.own(part), self.me, part, mask, 2 * mask + part)

    def relay(self, stage):
        if self.count == 8:
            if stage == 0:
                self.pass_on(2, 0, 0, 6, 4)
                self.pass_on(4, 1, 1, 8, 2)
                self.pass_on(2, 0, None, 7, 1)
                self.pass_on(4, 1, None, 9, 1)
            elif stage == 1:
                self.pass_on(2, 1, 2, 10, 1)
                self.pass_on(4, 0, 3, 11, 1)
            else:
                self.pass_on(6, 0, 6, 12, 1)
                self.pass_on(6, 1, 8, 13, 1)
        elif stage == 2:
            for mask in range(2, self.count, 2):
                for part in range(2):
                    self.pass_on(mask, part, 2 * mask + part, 2 * mask + 2 + part, 1)

    def ready(self, masks):
        if self.count == 8:
            last = ((1, 0, 4), (1, 1, 5), (3, 0, 7), (5, 1, 9), (3, 1, 10), (5, 0, 11))
            last += ((7, 0, 12), (7, 1, 13))
        else:
            last = [(m, p, 2 * m + p) for m in range(1, self.count, 2) for p in range(2)]
        for mask, part, index in last:
            if mask in masks:
                self.arrived(self.near(mask), part, index)

    def finish(self, masks=None):
        self.ready(range(self.count) if masks is None else masks)
        for index in self.waiting:
            spot = self.slot(self.me, 0)
            remote(
                spot, spot, self.sends, self.recvs, index, (self.rep, self.me)
            ).wait_send()


PARTS = 8


def expert_kernel(count, reps, *refs):
    lined = reps == LINE
    (gate_ref, up_ref, down_ref), staging, refs = stage_in(refs, 3, 3)
    for copy in staging:
        copy.start()
    own_ref, slope_ref, mix_ref = refs[:3]
    refs = (None,) * 6 + refs[6:]
    hidden_out, grad_out, delta_out = refs[6:9]
    refs = refs[9:]
    if lined:
        line_out = refs[0]
        refs = refs[1:]
    (
        rows,
        slope_buf,
        hidden_buf,
        grad_buf,
        acc_both,
        acc_down,
        stage,
        send_sem,
        recv_sem,
        own_sem,
        slope_sem,
        hidden_sem,
        grad_sem,
        stage_sem,
    ) = refs[:14]
    rep = lax.axis_index("rep")
    me = lax.axis_index("shard")
    experts, width, hidden = gate_ref.shape
    tokens = own_ref.shape[0]
    half = tokens // 2
    low = jnp.bfloat16
    turns = experts * count
    swap = 2 + count

    def pair(t):
        late = jnp.where(t < swap, t - 2, t - count)
        return (
            jnp.where(t < 4, t // 2, late),
            jnp.where(t < 4, t % 2, jnp.where(t < swap, 0, 1)),
        )

    def pack_of(t):
        return flip(me, pair(t)[0], count)

    def slope_copy(t):
        return pltpu.make_async_copy(
            slope_ref.at[:, pack_of(t)], slope_buf.at[t % 2], slope_sem.at[t % 2]
        )

    def hidden_copy(t):
        spot = pl.ds(pl.multiple_of(pair(t)[1] * hidden, hidden), hidden)
        return pltpu.make_async_copy(
            hidden_buf.at[t % 2], hidden_out.at[pack_of(t), :, spot], hidden_sem.at[t % 2]
        )

    def grad_copy(t):
        spot = pl.ds(pl.multiple_of(pair(t)[1] * 2 * hidden, 2 * hidden), 2 * hidden)
        return pltpu.make_async_copy(
            grad_buf.at[t % 2], grad_out.at[pack_of(t), :, spot], grad_sem.at[t % 2]
        )

    def stage_copy(e):
        span = pl.ds(e * 3 * PARTS, 3 * PARTS)
        return pltpu.make_async_copy(stage.at[span], delta_out.at[span], stage_sem.at[e])

    slope_copy(0).start()
    own = pltpu.make_async_copy(own_ref, rows.at[me], own_sem)
    own.start()
    greet(me, rep, count, reps if lined else 1)
    gather = Gather(
        count,
        rep,
        me,
        lambda p: own_ref.at[pl.ds(p * half, half)],
        lambda owner, p: rows.at[owner, pl.ds(p * half, half)],
        send_sem,
        recv_sem,
    )
    gather.start()
    own.wait()
    for copy in staging:
        copy.wait()
    if lined:
        line = Line(rep, me, stage, line_out, *refs[14:], count=PARTS)

    def wrap_up(e):
        size = acc_down.shape[1] // PARTS
        side = acc_both.shape[1] // (2 * PARTS)
        base = e * 3 * PARTS
        for i in range(PARTS):
            down = base + (0 if e == 0 else 2 * PARTS) + i
            stage[down] = acc_down[e, i * size : (i + 1) * size, :].astype(low)
            for which in range(2):
                at = base + (PARTS if e == 0 else 0) + which * PARTS + i
                for piece in range(2):
                    span = slice((2 * i + piece) * side, (2 * i + piece + 1) * side)
                    stage[at, :, piece * hidden : (piece + 1) * hidden] = acc_both[
                        e, span, which * hidden : (which + 1) * hidden
                    ].astype(low)
        stage_copy(e).start()

    if count == 8:
        plan = {2: ((1,), 0), 4: ((), 1), 5: ((3,), None), 7: ((5,), 2), 9: ((7,), None)}
    else:
        plan = {2: ((1,), None), 4: ((), 2), 5: (tuple(range(3, count, 2)), None)}

    def step(t, carry):
        k, e = pair(t)
        pack = flip(me, k, count)
        for at, (masks, stage_at) in plan.items():

            @pl.when(t == at)
            def _():
                gather.ready(masks)
                if stage_at is not None:
                    gather.relay(stage_at)

        @pl.when(t + 1 < turns)
        def _():
            slope_copy(t + 1).start()

        if lined:
            line.ticks(2 * (t - swap - 1), 2 * (t - swap))
        slope_copy(t).wait()

        @pl.when(t >= 2)
        def _():
            hidden_copy(t - 2).wait()
            grad_copy(t - 2).wait()

        slot = t % 2
        x = rows[pack]
        dy = slope_buf[slot].reshape(tokens, width)
        mixes = jnp.transpose(mix_ref[pack])
        mix = jnp.where(e == 0, mixes[:, 0:1], mixes[:, 1:2])
        for part in range(hidden // TILE):
            span = pl.ds(part * TILE, TILE)
            ga = matmul(x, gate_ref[e, :, span], NN)
            ua = matmul(x, up_ref[e, :, span], NN)
            dh = matmul(dy, down_ref[e, span, :], NT) * mix
            sig = jax.nn.sigmoid(ga)
            act = ga * sig
            hidden_buf[slot, :, span] = (mix * (act * ua)).astype(low)
            grad_buf[slot, :, span] = (dh * ua * sig * (1.0 + ga * (1.0 - sig))).astype(low)
            grad_buf[slot, :, pl.ds(hidden + part * TILE, TILE)] = (dh * act).astype(low)
        hidden_copy(t).start()
        grad_copy(t).start()

        def add(acc, value):
            @pl.when(k == 0)
            def _():
                acc[e] = value

            @pl.when(k > 0)
            def _():
                acc[e] += value

        add(acc_both, matmul(x, grad_buf[slot], TN))
        add(acc_down, matmul(hidden_buf[slot], dy, TN))

        @pl.when(t == swap - 1)
        def _():
            wrap_up(0)
            if lined:
                line.start()

        return carry

    lax.fori_loop(0, turns, step, 0)
    wrap_up(1)
    if lined:
        line.ticks(2 * (turns - swap - 1), PARTS + LAG)
    for t in (turns - 2, turns - 1):
        hidden_copy(t).wait()
        grad_copy(t).wait()
    gather.finish(())
    stage_copy(0).wait()
    if lined:
        line.finish()
    stage_copy(1).wait()


def expert_pass(normed, all_slopes, mixing, gate_weight, up_weight, down_weight, count, reps):
    tokens, width = normed.shape
    experts, _, hidden = gate_weight.shape
    block = tokens // count
    low = jnp.bfloat16
    full = jnp.float32
    dma = pltpu.SemaphoreType.DMA
    vmem = pltpu.VMEM
    shape = jax.ShapeDtypeStruct
    anywhere = pl.BlockSpec(memory_space=pl.ANY)
    inside = pl.BlockSpec(memory_space=pltpu.VMEM)
    flops = 2 * count * tokens * width * hidden * experts * 6
    lined = reps == LINE
    segment = (hidden // PARTS, width)
    summed = (PARTS,) + segment
    return pl.pallas_call(
        functools.partial(expert_kernel, count, reps),
        name="expert_pass",
        out_shape=(
            shape((count, tokens, experts * hidden), low),
            shape((count, tokens, 2 * experts * hidden), low),
            shape((6 * PARTS,) + segment, low),
        )
        + ((shape(summed, low),) if lined else ()),
        in_specs=[anywhere, anywhere, inside, anywhere, anywhere, anywhere],
        out_specs=(anywhere,) * 3 + ((inside,) if lined else ()),
        scratch_shapes=[
            vmem((count, tokens, width), low),
            vmem((2, count, block, width), low),
            vmem((2, tokens, hidden), low),
            vmem((2, tokens, 2 * hidden), low),
            vmem((experts, width, 2 * hidden), full),
            vmem((experts, hidden, width), full),
            vmem((6 * PARTS,) + segment, low),
            dma((2 * count + 2,)),
            dma((2 * count + 2,)),
            dma,
            dma((2,)),
            dma((2,)),
            dma((2,)),
            dma((2,)),
        ]
        + (line_scratch(summed, False) if lined else [])
        + [vmem(w.shape, low) for w in (gate_weight, up_weight, down_weight)]
        + [dma((3,))],
        compiler_params=pltpu.CompilerParams(
            collective_id=1, has_side_effects=True, vmem_limit_bytes=VMEM_MOST
        ),
        cost_estimate=pl.CostEstimate(flops=flops, bytes_accessed=1 << 26, transcendentals=0),
    )(
        normed,
        all_slopes.reshape(count, count, block, width),
        mixing,
        gate_weight,
        up_weight,
        down_weight,
    )


def return_kernel(count, reps, *refs):
    (gate_ref, up_ref, down_ref, own_ref), staging, refs = stage_in(refs, 4, 2)
    for copy in staging:
        copy.start()
    grad_ref, hidden_ref = refs[:2]
    lined = reps == LINE
    refs = refs[6:]
    if lined:
        line_ref, back_ref, piece_out, line_out = refs[:4]
        refs = refs[4:]
    else:
        back_ref, piece_out = refs[:2]
        refs = refs[2:]
    (
        grad_buf,
        hidden_buf,
        pair_send,
        far_send,
        pair_recv,
        far_recv,
        total,
        piece,
        last_recv,
        relay_recv,
        load_sem,
        pair_send_sem,
        pair_recv_sem,
        far_send_sem,
        far_recv_sem,
        piece_sem,
        last_sem,
        relay_send_sem,
        relay_recv_sem,
    ) = refs[:19]
    rep = lax.axis_index("rep")
    me = lax.axis_index("shard")
    experts, width, hidden = gate_ref.shape
    tokens = own_ref.shape[0]
    block = tokens // count
    low = jnp.bfloat16
    full = jnp.float32
    pairs = count // 2
    partner = flip(me, 1, count)
    line = Line(rep, me, line_ref, line_out, *refs[19:], base=PARTS, count=2 * PARTS) if lined else None

    relayed = count == 8
    half = tokens // 2

    def mask_of(turn):
        return count - 2 - 2 * turn

    def target(item):
        return flip(me, mask_of(item // 2) + 1 - item % 2, count)

    def grad_load(item):
        return pltpu.make_async_copy(
            grad_ref.at[target(item)], grad_buf.at[item % 2], load_sem.at[item % 2]
        )

    def grad_part(slot, pack):
        value = None
        for e in range(experts):
            for at, weight in ((2 * e, gate_ref), (2 * e + 1, up_ref)):
                term = matmul(grad_buf[slot, :, pl.ds(at * hidden, hidden)], weight[e], NT)
                value = term if value is None else value + term
        total[...] = value

    def hidden_load(item):
        return pltpu.make_async_copy(
            hidden_ref.at[:, target(item)], hidden_buf.at[item % 2], load_sem.at[item % 2]
        )

    def hidden_part(slot, pack):
        value = None
        for e in range(experts):
            term = matmul(
                hidden_buf[slot, :, :, pl.ds(e * hidden, hidden)].reshape(tokens, hidden),
                down_ref[e],
                NN,
            )
            value = term if value is None else value + term
        total[...] = value
        mine = pl.ds(pl.multiple_of(me * block, block), block)
        theirs = pl.ds(pl.multiple_of(pack * block, block), block)
        total[mine, :] += own_ref[theirs, :].astype(full)

    def pair_copy(base, turn):
        return remote(
            pair_send.at[turn % 2],
            pair_recv.at[base + turn],
            pair_send_sem,
            pair_recv_sem,
            base + turn,
            (rep, partner),
        )

    def far_copy(turn, device):
        return remote(
            far_send.at[turn % 2], far_recv.at[turn], far_send_sem, far_recv_sem, turn, (rep, device)
        )

    def half_copy(side):
        span = pl.ds(side * half, half)
        return remote(
            far_send.at[1, span],
            far_recv.at[1, span],
            far_send_sem,
            far_recv_sem,
            side,
            (rep, flip(me, count - 4, count)),
        )

    def relay_copy(phase, side, source):
        return remote(
            source.at[pl.ds(side * half, half)],
            relay_recv.at[2 * phase + side],
            relay_send_sem,
            relay_recv_sem,
            2 * phase + side,
            (rep, flip(me, 2 + 2 * side, count)),
        )

    def last_copy(device):
        return pltpu.make_async_remote_copy(
            src_ref=piece.at[0],
            dst_ref=last_recv,
            send_sem=last_sem.at[0],
            recv_sem=last_sem.at[1],
            device_id=(rep, device),
            device_id_type=MESH,
        )

    def slot(turn):
        return jnp.where(turn == 0, 0, jnp.where(turn == pairs - 1, 3, 1 + turn % 2))

    def piece_copy(turn):
        return pltpu.make_async_copy(
            piece.at[slot(turn)], piece_out.at[turn], piece_sem.at[turn % 2]
        )

    def grad_combine(turn, mask):
        last = turn == pairs - 1
        total[...] += pair_recv[turn].astype(full)

        @pl.when(last)
        def _():
            back_ref[...] = total[...]

        if relayed:

            @pl.when(turn == 0)
            def _():
                far_send[0] = total[...].astype(low)
                for side in range(2):
                    relay_copy(0, side, far_send.at[0]).start()

            @pl.when(turn == 1)
            def _():
                far_send[1] = total[...].astype(low)
                half_copy(1).start()

            @pl.when(turn == 2)
            def _():
                early, later = pl.ds(0, half), pl.ds(half, half)
                for side in range(2):
                    relay_copy(0, side, far_send.at[0]).wait_recv()
                value = far_send[1, early, :].astype(full) + relay_recv[0].astype(full)
                far_send[1, early, :] = value.astype(low)
                half_copy(0).start()
                for side in range(2):
                    relay_copy(0, side, far_send.at[0]).wait_send()
                total[later, :] += relay_recv[1].astype(full)
                far_send[0] = total[...].astype(low)
                far_copy(2, flip(me, mask, count)).start()
        else:

            @pl.when(jnp.logical_not(last))
            def _():
                @pl.when(turn >= 2)
                def _():
                    far_copy(turn - 2, me).wait_send()

                far_send[turn % 2] = total[...].astype(low)
                far_copy(turn, flip(me, mask, count)).start()

    def hidden_combine(turn, mask):
        if not relayed:

            @pl.when((turn >= 3) & (turn < pairs - 1))
            def _():
                piece_copy(turn - 2).wait()

        piece[slot(turn)] = (total[...] + pair_recv[pairs + turn].astype(full)).astype(low)

        @pl.when(turn == 0)
        def _():
            if relayed:
                for side in range(2):
                    relay_copy(1, side, piece.at[0]).start()
            else:
                last_copy(flip(me, mask, count)).start()

        if not relayed:

            @pl.when((turn > 0) & (turn < pairs - 1))
            def _():
                piece_copy(turn).start()

    grad_load(0).start()
    greet(me, rep, count, reps if lined else 1)
    if lined:
        line.start()

    def sweep(base, load, part, combine, before):
        def item_step(item, carry):
            turn = item // 2
            mask = mask_of(turn)

            @pl.when(item + 1 < 2 * pairs)
            def _():
                load(item + 1).start()

            load(item).wait()
            part(item % 2, target(item))

            @pl.when(item % 2 == 0)
            def _():
                @pl.when(turn >= 2)
                def _():
                    pair_copy(base, turn - 2).wait_send()

                pair_send[turn % 2] = total[...].astype(low)
                pair_copy(base, turn).start()

            @pl.when(item % 2 == 1)
            def _():
                pair_copy(base, turn).wait_recv()
                combine(turn, mask)

            if lined:
                line.tick(before + item - 2)
            return carry

        lax.fori_loop(0, 2 * pairs, item_step, 0)
        for turn in range(max(0, pairs - 2), pairs):
            pair_copy(base, turn).wait_send()

    for copy in staging:
        copy.wait()
    sweep(0, grad_load, grad_part, grad_combine, 0)
    hidden_load(0).start()
    sweep(pairs, hidden_load, hidden_part, hidden_combine, 2 * pairs)
    if lined:
        line.ticks(4 * pairs - 2, 2 * PARTS - 1)
    if relayed:
        for side in range(2):
            half_copy(side).wait_recv()
        back_ref[...] += far_recv[1].astype(full)
        far_copy(2, me).wait_recv()
        back_ref[...] += far_recv[2].astype(full)
        for side in range(2):
            half_copy(side).wait_send()
        far_copy(2, me).wait_send()
    else:

        def add(turn, carry):
            far_copy(turn, me).wait_recv()
            back_ref[...] += far_recv[turn].astype(full)
            return carry

        lax.fori_loop(0, pairs - 1, add, 0)
        for turn in (pairs - 3, pairs - 2):
            far_copy(turn, me).wait_send()
    if lined:
        line.ticks(2 * PARTS - 1, 2 * PARTS + LAG)
    if relayed:
        for side in range(2):
            relay_copy(1, side, piece.at[0]).wait_recv()
            rows = pl.ds(side * half, half)
            spot = slot(1 + side)
            value = piece[spot, rows, :].astype(full) + relay_recv[2 + side].astype(full)
            piece[spot, rows, :] = value.astype(low)
            piece_copy(1 + side).start()
            relay_copy(1, side, piece.at[0]).wait_send()
    else:
        last_copy(me).wait_recv()
        value = piece[3].astype(full) + last_recv[...].astype(full)
        piece[3] = value.astype(low)
        last_copy(me).wait_send()
    for turn in (pairs - 3, pairs - 2):
        piece_copy(turn).wait()
    piece_copy(pairs - 1).start()
    if lined:
        line.finish()
    piece_copy(pairs - 1).wait()


def return_pass(grads, hiddens, gate_weight, up_weight, down_weight, own, deltas, count, reps):
    tokens, width = own.shape
    experts, _, hidden = gate_weight.shape
    block = tokens // count
    low = jnp.bfloat16
    full = jnp.float32
    pairs = count // 2
    dma = pltpu.SemaphoreType.DMA
    shape = jax.ShapeDtypeStruct
    anywhere = pl.BlockSpec(memory_space=pl.ANY)
    inside = pl.BlockSpec(memory_space=pltpu.VMEM)
    flops = 2 * count * tokens * width * hidden * experts * 3
    lined = reps == LINE
    extra = [deltas] if lined else []
    return pl.pallas_call(
        functools.partial(return_kernel, count, reps),
        name="return_pass",
        out_shape=(
            shape((tokens, width), full),
            shape((pairs, tokens, width), low),
        )
        + tuple(shape((2 * PARTS,) + d.shape[1:], low) for d in extra),
        in_specs=[anywhere] * (6 + len(extra)),
        out_specs=(inside, anywhere) + (anywhere,) * len(extra),
        scratch_shapes=[
            pltpu.VMEM((2, tokens, 2 * experts * hidden), low),
            pltpu.VMEM((2, count, block, experts * hidden), low),
            pltpu.VMEM((2, tokens, width), low),
            pltpu.VMEM((2, tokens, width), low),
            pltpu.VMEM((2 * pairs, tokens, width), low),
            pltpu.VMEM((pairs, tokens, width), low),
            pltpu.VMEM((tokens, width), full),
            pltpu.VMEM((4, tokens, width), low),
            pltpu.VMEM((8, 128) if count == 8 else (tokens, width), low),
            pltpu.VMEM((4, tokens // 2, width), low),
            dma((2,)),
            dma((2 * pairs,)),
            dma((2 * pairs,)),
            dma((pairs,)),
            dma((pairs,)),
            dma((2,)),
            dma((3,)),
            dma((4,)),
            dma((4,)),
        ]
        + (line_scratch((2 * PARTS,) + deltas.shape[1:]) if lined else [])
        + [pltpu.VMEM(a.shape, low) for a in (gate_weight, up_weight, down_weight, own)]
        + [dma((4,))],
        compiler_params=pltpu.CompilerParams(
            collective_id=2, has_side_effects=True, vmem_limit_bytes=VMEM_MOST
        ),
        cost_estimate=pl.CostEstimate(flops=flops, bytes_accessed=1 << 26, transcendentals=0),
    )(
        grads,
        hiddens.reshape(count, count, block, experts * hidden),
        gate_weight,
        up_weight,
        down_weight,
        own,
        *extra,
    )


def turn_pairs(rows, along, across, sign):
    lane = lax.broadcasted_iota(jnp.int32, (rows.shape[0], 128), 1)
    early = (lane % HEAD_SIZE) < HEAD_SIZE // 2
    pieces = []
    for at in range(0, rows.shape[1], 128):
        part = rows[:, at : at + 128]
        other = jnp.where(
            early,
            pltpu.roll(part, 128 - HEAD_SIZE // 2, 1),
            pltpu.roll(part, HEAD_SIZE // 2, 1),
        )
        pieces.append(part * along + sign * (other * across))
    return pieces[0] if len(pieces) == 1 else jnp.concatenate(pieces, axis=1)


def permutation(order_ref):
    tokens = order_ref.shape[1]
    rows = lax.broadcasted_iota(jnp.int32, (tokens, tokens), 0)
    return jnp.where(order_ref[...] == rows, 1.0, 0.0).astype(jnp.bfloat16)


def starts_of(position, length_ref):
    start = jnp.zeros_like(position)
    end = jnp.zeros((1, 1), jnp.int32)
    for k in range(length_ref.shape[1] - 1):
        end = end + length_ref[0:1, k : k + 1]
        start = jnp.where(position >= end, end, start)
    return start


def fill_bias(bias, length_ref):
    tokens = bias.shape[0]
    keys = lax.broadcasted_iota(jnp.int32, (tokens, tokens), 0)
    queries = lax.broadcasted_iota(jnp.int32, (tokens, tokens), 1)
    start = starts_of(lax.broadcasted_iota(jnp.int32, (1, tokens), 1), length_ref)
    bias[...] = jnp.where((keys >= start) & (keys <= queries), 0.0, -1e30)


def query_spans(tokens):
    half = tokens // 2
    return ((0, half, half), (half, half, tokens))


def first_kernel(
    count,
    token_ref,
    query_ref,
    key_ref,
    value_ref,
    output_ref,
    gain_ref,
    order_ref,
    id_ref,
    gate_ref,
    arrived_out,
    joined_out,
    gain_out,
    mix_out,
    mix_buf,
    gain_buf,
    token_send,
    token_recv,
    gain_send,
    gain_recv,
    mix_send,
    mix_recv,
    weight_send,
    weight_recv,
    local_sem,
):
    rep = lax.axis_index("rep")
    me = lax.axis_index("shard")
    full = jnp.float32
    low = jnp.bfloat16
    rows = query_ref.shape[0]
    experts = mix_out.shape[0] * 2
    mine = pl.multiple_of(me * rows, rows)
    locals_ = [pltpu.make_async_copy(token_ref.at[me], arrived_out.at[me], local_sem.at[0])]
    at = 0
    for i, ref in enumerate((query_ref, key_ref, value_ref, output_ref)):
        size = ref.shape[1]
        target = joined_out.at[pl.ds(mine, rows), pl.ds(at, size)]
        locals_.append(pltpu.make_async_copy(ref, target, local_sem.at[1 + i]))
        at += size
    for copy in locals_:
        copy.start()
    greet(me, rep, count)

    def token_copy(k):
        target = flip(me, k, count)
        return remote(
            token_ref.at[target], arrived_out.at[me], token_send, token_recv, k, (rep, target)
        )

    def gain_copy(k):
        return remote(
            gain_ref, gain_buf.at[me], gain_send, gain_recv, k, (rep, flip(me, k, count))
        )

    def mix_copy(k):
        target = flip(me, k, count)
        return remote(mix_buf.at[target], mix_out.at[me], mix_send, mix_recv, k, (rep, target))

    for k in range(count - 1, 0, -1):
        token_copy(k).start()
    for copy in locals_[1:]:
        copy.wait()
    half = rows // 2

    def block(owner, part):
        return joined_out.at[pl.ds(pl.multiple_of(owner * rows + part * half, half), half)]

    weights = Gather(count, rep, me, lambda p: block(me, p), block, weight_send, weight_recv)
    weights.start()
    for k in range(1, count):
        gain_copy(k).start()
    gain_buf[me] = gain_ref[...]
    tokens = order_ref.shape[0]
    lane = lax.broadcasted_iota(jnp.int32, (tokens, experts), 1)
    mixing = jnp.zeros((tokens, experts), full)
    for k in range(id_ref.shape[1]):
        mixing = mixing + jnp.where(id_ref[:, k : k + 1] == lane, gate_ref[:, k : k + 1], 0.0)
    place = permutation(order_ref)
    moved = jnp.zeros((experts, tokens), full)
    for _ in range(3):
        high = mixing.astype(low)
        moved = moved + matmul(high, place, TN)
        mixing = mixing - high.astype(full)
    for owner in range(count):
        mix_buf[owner, 0:2, :] = moved[2 * owner : 2 * owner + 2, :]
        mix_buf[owner, 2:8, :] = jnp.zeros((6, tokens), full)
    weights.relay(0)
    for k in range(1, count):
        mix_copy(k).start()
    mix_out[me] = mix_buf[me]
    weights.relay(1)
    weights.relay(2)
    locals_[0].wait()
    for k in range(1, count):
        gain_copy(k).wait_recv()
    for owner in range(count):
        gain_out[:, owner * rows : (owner + 1) * rows] = gain_buf[owner]
    for k in range(1, count):
        token_copy(k).wait_recv()
        mix_copy(k).wait_recv()
    weights.finish()
    for k in range(1, count):
        token_copy(k).wait_send()
        gain_copy(k).wait_send()
        mix_copy(k).wait_send()


def first_pass(tokens, weights, gains, order, expert_ids, gates, count):
    rows = weights[0].shape[0]
    number, width = tokens.shape
    block = number // count
    low = jnp.bfloat16
    full = jnp.float32
    dma = pltpu.SemaphoreType.DMA
    inside = pl.BlockSpec(memory_space=pltpu.VMEM)
    columns = sum(w.shape[1] for w in weights)
    shape = jax.ShapeDtypeStruct
    return pl.pallas_call(
        functools.partial(first_kernel, count),
        name="first_pass",
        out_shape=(
            shape((count, block, width), low),
            shape((rows * count, columns), low),
            shape((8, rows * count), full),
            shape((count, 8, number), full),
        ),
        in_specs=[inside] * 9,
        out_specs=(inside,) * 4,
        scratch_shapes=[
            pltpu.VMEM((count, 8, number), full),
            pltpu.VMEM((count, 8, rows), full),
            dma((count,)),
            dma((count,)),
            dma((count,)),
            dma((count,)),
            dma((count,)),
            dma((count,)),
            dma((2 * count + 2,)),
            dma((2 * count + 2,)),
            dma((5,)),
        ],
        compiler_params=pltpu.CompilerParams(
            collective_id=4, has_side_effects=True, vmem_limit_bytes=VMEM_MOST
        ),
        cost_estimate=pl.CostEstimate(flops=1 << 24, bytes_accessed=1 << 26, transcendentals=0),
    )(tokens.reshape(count, block, width), *weights, gains, order, expert_ids, gates)


def front_kernel(
    count,
    token_ref,
    query_ref,
    key_ref,
    value_ref,
    output_ref,
    first_ref,
    second_ref,
    order_ref,
    id_ref,
    gate_ref,
    length_ref,
    speed_ref,
    cotangent_ref,
    joined_out,
    gain_out,
    mix_out,
    along_out,
    across_out,
    input_out,
    query_out,
    key_out,
    value_out,
    mixed_out,
    logsum_out,
    hidden_out,
    normed_out,
    shared_out,
    slopes_out,
    arrived,
    joined,
    mix_buf,
    gain_src,
    gain_buf,
    place,
    bias,
    normed,
    inputs,
    projected,
    mixed,
    hidden,
    moved,
    shared,
    token_send,
    token_recv,
    gain_send,
    gain_recv,
    mix_send,
    mix_recv,
    weight_send,
    weight_recv,
    slope_send,
    slope_recv,
    local_sem,
    out_sem,
):
    rep = lax.axis_index("rep")
    me = lax.axis_index("shard")
    low = jnp.bfloat16
    full = jnp.float32
    rows = query_ref.shape[0]
    tokens, width = cotangent_ref.shape
    key_width = key_ref.shape[1]
    experts = mix_out.shape[0] * 2
    mine = pl.multiple_of(me * rows, rows)
    own = [pltpu.make_async_copy(token_ref.at[me], arrived.at[me], local_sem.at[0])]
    at = 0
    for i, ref in enumerate((query_ref, key_ref, value_ref, output_ref)):
        size = ref.shape[1]
        spot = joined.at[pl.ds(mine, rows), pl.ds(at, size)]
        own.append(pltpu.make_async_copy(ref, spot, local_sem.at[1 + i]))
        at += size
    own.append(pltpu.make_async_copy(cotangent_ref, slopes_out.at[me], local_sem.at[5]))
    for copy in own:
        copy.start()
    gain_src[...] = jnp.zeros(gain_src.shape, full)
    gain_src[0:1, :] = first_ref[...].astype(full)
    gain_src[1:2, :] = second_ref[...].astype(full)
    greet(me, rep, count)

    def token_copy(k):
        target = flip(me, k, count)
        return remote(
            token_ref.at[target], arrived.at[me], token_send, token_recv, k, (rep, target)
        )

    def gain_copy(k):
        return remote(
            gain_src, gain_buf.at[me], gain_send, gain_recv, k, (rep, flip(me, k, count))
        )

    def mix_copy(k):
        target = flip(me, k, count)
        return remote(mix_buf.at[target], mix_out.at[me], mix_send, mix_recv, k, (rep, target))

    for k in range(count - 1, 0, -1):
        token_copy(k).start()
    for copy in own[1:5]:
        copy.wait()
    half = rows // 2

    def block(owner, part):
        return joined.at[pl.ds(pl.multiple_of(owner * rows + part * half, half), half)]

    weights = Gather(count, rep, me, lambda p: block(me, p), block, weight_send, weight_recv)
    weights.start()
    for k in range(1, count):
        gain_copy(k).start()
    gain_buf[me] = gain_src[...]
    some = tokens // 2
    slopes = Gather(
        count,
        rep,
        me,
        lambda p: cotangent_ref.at[pl.ds(p * some, some)],
        lambda owner, p: slopes_out.at[owner, pl.ds(p * some, some)],
        slope_send,
        slope_recv,
    )
    kinds = lax.broadcasted_iota(jnp.int32, (experts, tokens), 0)
    mixing = jnp.zeros((experts, tokens), full)
    for k in range(id_ref.shape[0]):
        mixing = mixing + jnp.where(id_ref[k : k + 1, :] == kinds, gate_ref[k : k + 1, :], 0.0)
    place[...] = permutation(order_ref)
    dealt = jnp.zeros((experts, tokens), full)
    for _ in range(3):
        high = mixing.astype(low)
        dealt = dealt + matmul(high, place[...], NT)
        mixing = mixing - high.astype(full)
    for owner in range(count):
        mix_buf[owner, 0:2, :] = dealt[2 * owner : 2 * owner + 2, :]
        mix_buf[owner, 2:8, :] = jnp.zeros((6, tokens), full)
    weights.relay(0)
    for k in range(1, count):
        mix_copy(k).start()
    mix_out[me] = mix_buf[me]
    slopes.start()
    fill_bias(bias, length_ref)
    position = lax.broadcasted_iota(jnp.int32, along_out.shape, 0)
    angle = (position - starts_of(position, length_ref)).astype(full) * speed_ref[0:1, :]
    along_out[...] = jnp.cos(angle)
    across_out[...] = jnp.sin(angle) * speed_ref[1:2, :]
    own[0].wait()
    for k in range(1, count):
        token_copy(k).wait_recv()
        gain_copy(k).wait_recv()
    for owner in range(count):
        gain_out[:, owner * rows : (owner + 1) * rows] = gain_buf[owner]
    outs = (
        (inputs, input_out),
        (projected.at[:, pl.ds(0, width)], query_out),
        (projected.at[:, pl.ds(width, key_width)], key_out),
        (projected.at[:, pl.ds(width + key_width, key_width)], value_out),
        (mixed, mixed_out),
        (hidden, hidden_out),
        (moved, normed_out),
        (shared, shared_out),
        (joined, joined_out),
    )
    puts = [pltpu.make_async_copy(a, b, out_sem.at[k]) for k, (a, b) in enumerate(outs)]
    rows_in = matmul(place[...], arrived[...].reshape(tokens, width), TN)
    inputs[...] = rows_in.astype(low)
    scale = lax.rsqrt(jnp.mean(rows_in * rows_in, axis=1, keepdims=True) + EPS)
    normed[...] = (rows_in * scale * gain_out[0:1, :]).astype(low)
    puts[0].start()
    weights.relay(1)
    weights.relay(2)
    weights.ready(range(count))
    puts[8].start()
    along = along_out[...]
    across = across_out[...]

    def turned(at, carry):
        spot = pl.ds(pl.multiple_of(at * key_width, key_width), key_width)
        part = matmul(normed[...], joined[:, spot], NN)
        projected[:, spot] = turn_pairs(part, along, across, 1.0).astype(low)
        return carry

    lax.fori_loop(0, width // key_width + 1, turned, 0)
    part = matmul(normed[...], joined[:, width + key_width : width + 2 * key_width], NN)
    projected[:, width + key_width :] = part.astype(low)
    for copy in puts[1:4]:
        copy.start()

    def heads(g, carry):
        qs = pl.ds(pl.multiple_of(g * 256, 256), 256)
        kv = pl.ds(pl.multiple_of(width + g * 128, 128), 128)
        keys = projected[:, kv]
        kv = pl.ds(pl.multiple_of(width + key_width + g * 128, 128), 128)
        values = projected[:, kv]
        queries = projected[:, qs] * jnp.bfloat16(HEAD_SIZE**-0.5)
        for start, size, reach in query_spans(tokens):
            pieces = []
            for h in range(4):
                a = (h // 2) * HEAD_SIZE
                score = matmul(
                    keys[:reach, a : a + HEAD_SIZE],
                    queries[start : start + size, h * HEAD_SIZE : (h + 1) * HEAD_SIZE],
                    NT,
                )
                score = score + bias[:reach, start : start + size]
                largest = jnp.max(score, axis=0, keepdims=True)
                powers = jnp.exp(score - largest)
                totals = jnp.sum(powers, axis=0, keepdims=True)
                shares = (powers * (1.0 / totals)).astype(low)
                pieces.append(matmul(shares, values[:reach, a : a + HEAD_SIZE], TN))
                logsum_out[g, h : h + 1, start : start + size] = largest + jnp.log(totals)
            mixed[start : start + size, qs] = jnp.concatenate(pieces, axis=1).astype(low)

        @pl.when(g == 1)
        def _():
            slopes.relay(0)

        return carry

    lax.fori_loop(0, key_width // 128, heads, 0)
    puts[4].start()
    total = inputs[...].astype(full) + matmul(mixed[...], joined[:, width + 2 * key_width :], NN)
    hidden[...] = total
    scale = lax.rsqrt(jnp.mean(total * total, axis=1, keepdims=True) + EPS)
    normed[...] = (total * scale * gain_out[1:2, :]).astype(low)
    puts[5].start()
    moved[...] = matmul(place[...], normed[...], NN).astype(low)
    puts[6].start()
    shared[...] = matmul(place[...], hidden[...].astype(low), NN).astype(low)
    puts[7].start()
    slopes.relay(1)
    for k in range(1, count):
        mix_copy(k).wait_recv()
    for copy in puts:
        copy.wait()
    slopes.relay(2)
    own[5].wait()
    slopes.finish()
    weights.finish(())
    for k in range(1, count):
        token_copy(k).wait_send()
        gain_copy(k).wait_send()
        mix_copy(k).wait_send()


def front_pass(tokens, weights, gains, order, expert_ids, gates, lengths, cotangent, count):
    rows = weights[0].shape[0]
    number, width = tokens.shape
    key_width = weights[1].shape[1]
    block = number // count
    low = jnp.bfloat16
    full = jnp.float32
    dma = pltpu.SemaphoreType.DMA
    vmem = pltpu.VMEM
    anywhere = pl.BlockSpec(memory_space=pl.ANY)
    inside = pl.BlockSpec(memory_space=pltpu.VMEM)
    columns = sum(w.shape[1] for w in weights)
    shape = jax.ShapeDtypeStruct
    half = HEAD_SIZE // 2
    speed = np.tile(THETA ** (-2.0 * np.arange(half) / HEAD_SIZE), 128 // half)
    side = np.tile(np.repeat([-1.0, 1.0], half), 128 // HEAD_SIZE)
    speeds = jnp.asarray(np.stack([speed, side]).astype(np.float32))
    return pl.pallas_call(
        functools.partial(front_kernel, count),
        name="front_pass",
        out_shape=(
            shape((rows * count, columns), low),
            shape((8, rows * count), full),
            shape((count, 8, number), full),
            shape((number, 128), full),
            shape((number, 128), full),
            shape((number, width), low),
            shape((number, width), low),
            shape((number, key_width), low),
            shape((number, key_width), low),
            shape((number, width), low),
            shape((key_width // 128, 4, number), full),
            shape((number, width), full),
            shape((number, width), low),
            shape((number, width), low),
            shape((count, number, width), low),
        ),
        in_specs=[anywhere] * 5 + [inside] * 7 + [anywhere],
        out_specs=(anywhere,)
        + (inside,) * 4
        + (anywhere,) * 5
        + (inside,)
        + (anywhere,) * 4,
        scratch_shapes=[
            vmem((count, block, width), low),
            vmem((rows * count, columns), low),
            vmem((count, 8, number), full),
            vmem((8, rows), full),
            vmem((count, 8, rows), full),
            vmem((number, number), low),
            vmem((number, number), full),
            vmem((number, width), low),
            vmem((number, width), low),
            vmem((number, width + 2 * key_width), low),
            vmem((number, width), low),
            vmem((number, width), full),
            vmem((number, width), low),
            vmem((number, width), low),
            dma((count,)),
            dma((count,)),
            dma((count,)),
            dma((count,)),
            dma((count,)),
            dma((count,)),
            dma((2 * count + 2,)),
            dma((2 * count + 2,)),
            dma((2 * count + 2,)),
            dma((2 * count + 2,)),
            dma((6,)),
            dma((9,)),
        ],
        compiler_params=pltpu.CompilerParams(
            collective_id=4, has_side_effects=True, vmem_limit_bytes=VMEM_MOST
        ),
        cost_estimate=pl.CostEstimate(
            flops=12 << 30, bytes_accessed=1 << 26, transcendentals=1 << 22
        ),
    )(
        tokens.reshape(count, block, width),
        *weights,
        *(gain.reshape(1, rows) for gain in gains),
        order,
        expert_ids.T,
        gates.T,
        lengths,
        speeds,
        cotangent,
    )


def finish_kernel(count, reps, *refs):
    lined = reps == LINE
    (
        back_ref,
        slopes_ref,
        order_ref,
        length_ref,
        along_ref,
        across_ref,
        weight_ref,
        gain_ref,
        input_ref,
        query_ref,
        key_ref,
        value_ref,
        mixed_ref,
        logsum_ref,
        hidden_ref,
        piece_ref,
    ) = refs[:16]
    refs = refs[16:]
    staged = (
        back_ref,
        hidden_ref,
        mixed_ref,
        weight_ref,
        query_ref,
        key_ref,
        value_ref,
        input_ref,
    )
    held = refs[-len(staged) - 1 : -1]
    staging = [
        pltpu.make_async_copy(ref, buf, refs[-1].at[k])
        for k, (ref, buf) in enumerate(zip(staged, held, strict=True))
    ]
    refs = refs[: -len(staged) - 1]
    (
        back_ref,
        hidden_ref,
        mixed_ref,
        weight_ref,
        query_ref,
        key_ref,
        value_ref,
        input_ref,
    ) = held
    if lined:
        line_ref = refs[0]
        refs = refs[1:]
    delta_out, gain_out, slope_out, out_ref = refs[:4]
    refs = refs[4:]
    if lined:
        line_out = refs[0]
        refs = refs[1:]
    (
        place,
        bias,
        normed,
        steep,
        mixed_slope,
        backs,
        arrived,
        far_piece,
        far_piece_send,
        far_piece_recv,
        local_sem,
        delta,
        pair_recv,
        far_send,
        far_recv,
        pair_send_sem,
        pair_recv_sem,
        far_send_sem,
        far_recv_sem,
        slope_send_sem,
        slope_recv_sem,
        gain_buf,
        gain_recv,
        gain_sum,
        gain_line,
        gain_send_sem,
        gain_recv_sem,
        gain_line_send,
        gain_line_recv,
        owned,
    ) = refs[:30]
    refs = refs[30:]
    low = jnp.bfloat16
    full = jnp.float32
    rep = lax.axis_index("rep")
    me = lax.axis_index("shard")
    pairs = count // 2
    partner = flip(me, 1, count)
    tokens, width = back_ref.shape
    key_width = key_ref.shape[1]
    joined = width + 2 * key_width
    rows = width // count
    block = tokens // count
    own_slopes = pltpu.make_async_copy(
        slopes_ref.at[:, pl.ds(pl.multiple_of(me * block, block), block)],
        arrived,
        local_sem.at[0],
    )
    staging[0].start()
    own_slopes.start()
    for copy in staging[1:]:
        copy.start()
    own_piece = pltpu.make_async_copy(piece_ref.at[pairs - 1], mixed_slope, local_sem.at[1])
    greet(me, rep, count, reps)
    if lined:
        line = Line(rep, me, line_ref, line_out, *refs[:7], base=3 * PARTS, count=3 * PARTS)
        sums = Line(rep, me, owned, delta_out, *refs[7:12])
        line.start()
    else:
        spread, spread_send, spread_recv = refs

    def tick(begin, end):
        if lined:
            line.ticks(begin, end)

    def piece_copy(turn):
        return remote(
            piece_ref.at[turn],
            far_piece.at[turn - 1],
            far_piece_send,
            far_piece_recv,
            turn,
            (rep, flip(me, count - 2 - 2 * turn, count)),
        )

    def rows_of(owner):
        return pl.ds(pl.multiple_of(owner * rows, rows), rows)

    columns = (slice(joined, joined + width), slice(0, joined))

    def pair_copy(part, turn):
        return remote(
            delta.at[rows_of(flip(partner, 2 * turn, count)), columns[part]],
            pair_recv.at[turn, :, columns[part]],
            pair_send_sem,
            pair_recv_sem,
            part * pairs + turn,
            (rep, partner),
        )

    def far_copy(part, turn):
        return remote(
            far_send.at[turn - 1, :, columns[part]],
            far_recv.at[turn - 1, :, columns[part]],
            far_send_sem,
            far_recv_sem,
            part * pairs + turn,
            (rep, flip(me, 2 * turn, count)),
        )

    def exchange(part):
        for turn in range(pairs - 1, -1, -1):
            pair_copy(part, turn).start()

    def combine(part):
        def step(i, carry):
            turn = pairs - 1 - i
            pair_copy(part, turn).wait_recv()
            mine = delta[rows_of(flip(me, 2 * turn, count)), columns[part]].astype(full)
            far_send[turn - 1, :, columns[part]] = (
                mine + pair_recv[turn, :, columns[part]].astype(full)
            ).astype(low)
            far_copy(part, turn).start()
            return carry

        lax.fori_loop(0, pairs - 1, step, 0)

    def collect(part, first, number):
        pair_copy(part, 0).wait_recv()
        for turn in range(1, pairs):
            far_copy(part, turn).wait_recv()
        half = rows // 2

        def step(i, carry):
            at = pl.ds(
                pl.multiple_of(columns[part].start + (i // 2) * width, width), width
            )
            span = pl.ds(pl.multiple_of((i % 2) * half, half), half)
            mine = pl.ds(pl.multiple_of(me * rows + (i % 2) * half, half), half)
            value = delta[mine, at].astype(full) + pair_recv[0, span, at].astype(full)
            for turn in range(1, pairs):
                value = value + far_recv[turn - 1, span, at].astype(full)
            owned[first + i] = value.astype(low)
            return carry

        lax.fori_loop(0, number, step, 0)

    def slope_copy(k):
        target = flip(me, k, count)
        return remote(
            arrived.at[target],
            slope_out.at[me],
            slope_send_sem,
            slope_recv_sem,
            k,
            (rep, target),
        )

    def gain_copy(k):
        target = flip(me, k, count)
        return remote(
            gain_buf.at[target], gain_recv.at[k], gain_send_sem, gain_recv_sem, k, (rep, target)
        )

    def gain_line_copy(k):
        return remote(
            gain_sum,
            gain_line.at[rep],
            gain_line_send,
            gain_line_recv,
            k,
            (lax.rem(rep + k, reps), me),
        )

    for turn in range(1, pairs - 1):
        piece_copy(turn).start()
    place[...] = permutation(order_ref)
    fill_bias(bias, length_ref)
    own_slopes.wait()
    staging[0].wait()
    high = back_ref[...].astype(low)
    rest = (back_ref[...] - high.astype(full)).astype(low)
    slope = matmul(place[...], high, TN) + matmul(place[...], rest, TN)
    steep[...] = slope
    tick(0, 1)
    slope = steep[...]
    staging[1].wait()
    hidden = hidden_ref[...]
    scale = lax.rsqrt(jnp.mean(hidden * hidden, axis=1, keepdims=True) + EPS)
    scaled = slope * gain_ref[1:2, :]
    second = jnp.sum(slope * hidden * scale, axis=0, keepdims=True)
    for owner in range(count):
        gain_buf[owner, 1:2, :] = second[:, owner * rows : (owner + 1) * rows]
    tick(1, 2)
    steep[...] = (
        matmul(place[...], arrived[...].reshape(tokens, width), TN)
        + scale * scaled
        - hidden * (scale * scale * scale) * jnp.mean(hidden * scaled, axis=1, keepdims=True)
    )
    tick(2, 3)
    sharp = steep[...].astype(low)
    staging[2].wait()
    normed[...] = sharp

    def output_part(at, carry):
        spot = pl.ds(pl.multiple_of(at * 512, 512), 512)
        to = pl.ds(pl.multiple_of(joined + at * 512, 512), 512)
        delta[:, to] = matmul(mixed_ref[...], normed[:, spot], TN).astype(low)
        return carry

    lax.fori_loop(0, width // 512, output_part, 0)
    exchange(0)
    tick(3, 4)
    staging[3].wait()
    mixed_slope[...] = matmul(sharp, weight_ref[:, joined:], NT).astype(low)
    tick(4, 5)
    along = along_ref[...]
    across = across_ref[...]

    def heads(g, carry):
        kv = pl.ds(pl.multiple_of(g * 128, 128), 128)
        qs = pl.ds(pl.multiple_of(g * 256, 256), 256)
        keys = key_ref[:, kv]
        values = value_ref[:, kv]
        queries = query_ref[:, qs] * jnp.bfloat16(HEAD_SIZE**-0.5)
        slopes = mixed_slope[:, qs]
        key_parts = []
        value_parts = []
        query_parts = [[], []]
        for a in range(2):
            tick(5 + 2 * g + a, 6 + 2 * g + a)
            key_h = keys[:, a * HEAD_SIZE : (a + 1) * HEAD_SIZE]
            value_h = values[:, a * HEAD_SIZE : (a + 1) * HEAD_SIZE]
            key_slope = [None, None]
            value_slope = [None, None]
            for b in range(2):
                h = 2 * a + b
                spot = slice(h * HEAD_SIZE, (h + 1) * HEAD_SIZE)
                for i, (start, size, reach) in enumerate(query_spans(tokens)):
                    q = queries[start : start + size, spot]
                    d = slopes[start : start + size, spot]
                    score = matmul(key_h[:reach], q, NT) + bias[:reach, start : start + size]
                    probs = jnp.exp(score - logsum_ref[g, h : h + 1, start : start + size])
                    prob_slope = matmul(value_h[:reach], d, NT)
                    inner = jnp.sum(probs * prob_slope, axis=0, keepdims=True)
                    score_slope = (probs * (prob_slope - inner)).astype(low)
                    term = matmul(probs.astype(low), d, NN)
                    value_slope[i] = term if b == 0 else value_slope[i] + term
                    term = matmul(score_slope, q, NN)
                    key_slope[i] = term if b == 0 else key_slope[i] + term
                    query_parts[i].append(matmul(score_slope, key_h[:reach], TN))
            half = tokens // 2
            key_parts.append(
                jnp.concatenate([key_slope[0] + key_slope[1][:half], key_slope[1][half:]], axis=0)
            )
            value_parts.append(
                jnp.concatenate(
                    [value_slope[0] + value_slope[1][:half], value_slope[1][half:]], axis=0
                )
            )
        for i, (start, size, reach) in enumerate(query_spans(tokens)):
            span = slice(start, start + size)
            part = jnp.concatenate(query_parts[i], axis=1) * HEAD_SIZE**-0.5
            backs[span, qs] = turn_pairs(part, along[span], across[span], -1.0).astype(low)
        part = jnp.concatenate(key_parts, axis=1)
        spot = pl.ds(pl.multiple_of(width + g * 128, 128), 128)
        backs[:, spot] = turn_pairs(part, along, across, -1.0).astype(low)
        part = jnp.concatenate(value_parts, axis=1)
        spot = pl.ds(pl.multiple_of(width + key_width + g * 128, 128), 128)
        backs[:, spot] = part.astype(low)

        @pl.when(g == 1)
        def _():
            combine(0)

        return carry

    for copy in staging[4:]:
        copy.wait()
    loops = key_width // 128
    lax.fori_loop(0, loops, heads, 0)
    done = 5 + 2 * loops
    own_piece.start()
    inputs = input_ref[...].astype(full)
    scale = lax.rsqrt(jnp.mean(inputs * inputs, axis=1, keepdims=True) + EPS)
    normed[...] = (inputs * scale * gain_ref[0:1, :]).astype(low)

    def input_part(at, carry):
        spot = pl.ds(pl.multiple_of(at * 512, 512), 512)
        delta[:, spot] = matmul(normed[...], backs[:, spot], TN).astype(low)
        return carry

    lax.fori_loop(0, joined // 512, input_part, 0)
    exchange(1)
    tick(done, done + 1)
    slope = matmul(backs[...], weight_ref[:, :joined], NT)
    combine(1)
    tick(done + 1, done + 2)
    scaled = slope * gain_ref[0:1, :]
    first = jnp.sum(slope * inputs * scale, axis=0, keepdims=True)
    for owner in range(count):
        gain_buf[owner, 0:1, :] = first[:, owner * rows : (owner + 1) * rows]
        gain_buf[owner, 2:8, :] = jnp.zeros((6, rows), full)
    for k in range(1, count):
        gain_copy(k).start()
    result = (
        steep[...]
        + scale * scaled
        - inputs * (scale * scale * scale) * jnp.mean(inputs * scaled, axis=1, keepdims=True)
    )
    moved = matmul(place[...], result.astype(low), NN).astype(low)
    arrived[...] = moved.reshape(arrived.shape)
    for k in range(count - 1, 0, -1):
        slope_copy(k).start()
    slope_out[me] = arrived[me]
    tick(done + 2, done + 5)
    own_piece.wait()
    result = mixed_slope[...].astype(full)
    for turn in range(1, pairs - 1):
        piece_copy(turn).wait_recv()
        result = result + far_piece[turn - 1].astype(full)
    out_ref[...] = result.astype(low)
    collect(0, 0, 2)
    if lined:
        sums.start(0, 2)
    total = gain_buf[me]
    for k in range(1, count):
        gain_copy(k).wait_recv()
        total = total + gain_recv[k]
    gain_sum[...] = total
    gain_line[rep] = total
    for k in range(1, reps):
        gain_line_copy(k).start()
    tick(done + 5, done + 9)
    collect(1, 2, 4)
    if lined:
        sums.start(2, 6)
        tick(done + 9, 3 * PARTS + LAG)
        sums.ticks(0, 6 + LAG)
        sums.finish()
    else:

        def spread_copy(k):
            return remote(
                owned, spread.at[rep], spread_send, spread_recv, k, (lax.rem(rep + k, reps), me)
            )

        for k in range(1, reps):
            spread_copy(k).start()
        spread[rep] = owned[...]
        for k in range(1, reps):
            spread_copy(k).wait_recv()
        value = spread[0].astype(full)
        for k in range(1, reps):
            value = value + spread[k].astype(full)
        delta_out[...] = value.astype(low)
        for k in range(1, reps):
            spread_copy(k).wait_send()
    for k in range(1, reps):
        gain_line_copy(k).wait_recv()
    total = gain_line[0]
    for k in range(1, reps):
        total = total + gain_line[k]
    gain_out[...] = total
    for k in range(1, count):
        slope_copy(k).wait_recv()
    for k in range(1, count):
        slope_copy(k).wait_send()
        gain_copy(k).wait_send()
    for turn in range(1, pairs - 1):
        piece_copy(turn).wait_send()
    for part in range(2):
        for turn in range(pairs):
            pair_copy(part, turn).wait_send()
        for turn in range(1, pairs):
            far_copy(part, turn).wait_send()
    for k in range(1, reps):
        gain_line_copy(k).wait_send()
    if lined:
        line.finish()


def finish_pass(count, reps, back, slopes, *rest):
    *rest, pieces, extra = rest
    tokens, width = back.shape
    weights = rest[4]
    key_width = (weights.shape[1] - 2 * width) // 2
    pairs = count // 2
    rows = width // count
    block = tokens // count
    columns = weights.shape[1]
    low = jnp.bfloat16
    full = jnp.float32
    dma = pltpu.SemaphoreType.DMA
    vmem = pltpu.VMEM
    shape = jax.ShapeDtypeStruct
    lined = reps == LINE
    extra = [extra] if lined else []
    owned = (2 * columns // width, rows // 2, width)
    anywhere = pl.BlockSpec(memory_space=pl.ANY)
    inside = pl.BlockSpec(memory_space=pltpu.VMEM)
    if lined:
        last = line_scratch((3 * PARTS,) + extra[0].shape[1:]) + line_scratch(owned, False)
    else:
        last = [vmem((reps,) + owned, low), dma((reps,)), dma((reps,))]
    return pl.pallas_call(
        functools.partial(finish_kernel, count, reps),
        name="finish_pass",
        out_shape=(
            shape(owned, low),
            shape((8, rows), full),
            shape((count, block, width), low),
            shape((tokens, width), low),
        )
        + tuple(shape((3 * PARTS,) + d.shape[1:], low) for d in extra),
        in_specs=[anywhere, anywhere]
        + [inside] * 4
        + [anywhere, inside]
        + [anywhere] * 5
        + [inside]
        + [anywhere] * (2 + len(extra)),
        out_specs=(inside,) * 4 + (anywhere,) * len(extra),
        scratch_shapes=[
            vmem((tokens, tokens), low),
            vmem((tokens, tokens), full),
            vmem((tokens, width), low),
            vmem((tokens, width), full),
            vmem((tokens, width), low),
            vmem((tokens, width + 2 * key_width), low),
            vmem((count, block, width), low),
            vmem((pairs - 2, tokens, width), low),
            dma((pairs,)),
            dma((pairs,)),
            dma((2,)),
            vmem((width, columns), low),
            vmem((pairs, rows, columns), low),
            vmem((pairs - 1, rows, columns), low),
            vmem((pairs - 1, rows, columns), low),
            dma((2 * pairs,)),
            dma((2 * pairs,)),
            dma((2 * pairs,)),
            dma((2 * pairs,)),
            dma((count,)),
            dma((count,)),
            vmem((count, 8, rows), full),
            vmem((count, 8, rows), full),
            vmem((8, rows), full),
            vmem((reps, 8, rows), full),
            dma((count,)),
            dma((count,)),
            dma((reps,)),
            dma((reps,)),
            vmem(owned, low),
        ]
        + last
        + [
            vmem(a.shape, a.dtype)
            for a in (back, rest[12], rest[10], weights, rest[7], rest[8], rest[9], rest[6])
        ]
        + [dma((8,))],
        compiler_params=pltpu.CompilerParams(
            collective_id=6, has_side_effects=True, vmem_limit_bytes=VMEM_MOST
        ),
        cost_estimate=pl.CostEstimate(
            flops=24 << 30, bytes_accessed=1 << 24, transcendentals=1 << 22
        ),
    )(back, slopes, *rest, pieces, *extra)


def emit_kernel(
    tokens_ref,
    slopes_ref,
    gain_ref,
    delta_ref,
    early_ref,
    middle_ref,
    late_ref,
    tokens_out,
    slopes_out,
    first_out,
    query_out,
    key_out,
    value_out,
    output_out,
    second_out,
    gate_out,
    up_out,
    down_out,
):
    full = jnp.float32
    tokens_out[...] = tokens_ref[...]
    slopes_out[...] = slopes_ref[...]
    rows = early_ref.shape[1]
    hidden = gate_out.shape[3]
    for piece in range(2):
        to = slice(piece * rows, (piece + 1) * rows)
        spot = slice(piece * hidden, (piece + 1) * hidden)
        gate_out[0, :, to, :] = middle_ref[0, :, :, spot].astype(full)
        up_out[0, :, to, :] = middle_ref[1, :, :, spot].astype(full)
        gate_out[1, :, to, :] = late_ref[0, :, :, spot].astype(full)
        up_out[1, :, to, :] = late_ref[1, :, :, spot].astype(full)
    down_out[0] = early_ref[...].astype(full)
    down_out[1] = late_ref[2].astype(full)

    @pl.when(pl.program_id(0) == 0)
    def _():
        first_out[...] = gain_ref[0:1, :]
        second_out[...] = gain_ref[1:2, :]
        half = delta_ref.shape[1]
        key_width = key_out.shape[1]
        for i in range(2):
            span = slice(i * half, (i + 1) * half)
            output_out[span, :] = delta_ref[i].astype(full)
            query_out[span, :] = delta_ref[2 + i].astype(full)
            key_out[span, :] = delta_ref[4 + i, :, :key_width].astype(full)
            value_out[span, :] = delta_ref[4 + i, :, key_width:].astype(full)


def emit_pass(tokens, slopes, gains, deltas, early, middle, late):
    full = jnp.float32
    shape = jax.ShapeDtypeStruct
    number, width = tokens.shape
    rows = gains.shape[1]
    _, high, wide = early.shape
    hidden = high * PARTS
    steps = 4
    each = PARTS // steps

    def moving(*block):
        return pl.BlockSpec(block, lambda i: (i,) + (0,) * (len(block) - 1))

    def fixed(*block):
        return pl.BlockSpec(block, lambda i: (0,) * len(block))

    def inner(*block):
        return pl.BlockSpec(block, lambda i: (0, i, 0, 0))

    return pl.pallas_call(
        emit_kernel,
        name="emit_pass",
        grid=(steps,),
        out_shape=(
            shape(tokens.shape, tokens.dtype),
            shape(slopes.shape, slopes.dtype),
            shape((1, rows), full),
            shape((rows, width), full),
            shape((rows, width // 2), full),
            shape((rows, width // 2), full),
            shape((rows, width), full),
            shape((1, rows), full),
            shape((2, PARTS, 2 * high, hidden), full),
            shape((2, PARTS, 2 * high, hidden), full),
            shape((2, PARTS, high, wide), full),
        ),
        in_specs=[
            moving(number // steps, width),
            moving(number // steps, width),
            fixed(*gains.shape),
            fixed(*deltas.shape),
            moving(each, high, wide),
            inner(2, each, high, wide),
            inner(3, each, high, wide),
        ],
        out_specs=(
            moving(number // steps, width),
            moving(number // steps, width),
            fixed(1, rows),
            fixed(rows, width),
            fixed(rows, width // 2),
            fixed(rows, width // 2),
            fixed(rows, width),
            fixed(1, rows),
            inner(2, each, 2 * high, hidden),
            inner(2, each, 2 * high, hidden),
            inner(2, each, high, wide),
        ),
        compiler_params=pltpu.CompilerParams(vmem_limit_bytes=VMEM_MOST),
        cost_estimate=pl.CostEstimate(flops=1 << 20, bytes_accessed=1 << 24, transcendentals=0),
    )(
        tokens,
        slopes,
        gains,
        deltas,
        early,
        middle.reshape(2, PARTS, high, wide),
        late.reshape(3, PARTS, high, wide),
    )


def local(
    tokens,
    cotangent,
    seq_lengths,
    pack_order,
    unpack_order,
    expert_ids,
    gates,
    first_gain,
    query_weight,
    key_matrix,
    value_matrix,
    output_weight,
    second_gain,
    gate_weight,
    up_weight,
    down_weight,
):
    shards = lax.axis_size("shard")
    group_count, width = tokens.shape
    order = pack_order.reshape(1, group_count)
    (
        joined,
        gains,
        mixing,
        along,
        across,
        inputs,
        queries,
        keys,
        values,
        mixed,
        logsum,
        hidden,
        normed,
        shared,
        all_slopes,
    ) = front_pass(
        tokens,
        (query_weight, key_matrix, value_matrix, output_weight),
        (first_gain, second_gain),
        order,
        expert_ids,
        gates,
        seq_lengths,
        cotangent,
        shards,
    )
    tables = (order, seq_lengths, along, across, joined, gains)
    reps = lax.axis_size("rep")
    inner, row_slopes, partial, *early = expert_pass(
        normed, all_slopes, mixing, gate_weight, up_weight, down_weight, shards, reps
    )
    back, pieces, *middle = return_pass(
        row_slopes, inner, gate_weight, up_weight, down_weight, shared, partial, shards, reps
    )
    deltas, gain_deltas, delta_tokens, out_tokens, *late = finish_pass(
        shards,
        reps,
        back,
        all_slopes,
        *tables,
        inputs,
        queries,
        keys,
        values,
        mixed,
        logsum,
        hidden,
        pieces,
        partial,
    )
    if reps == LINE:
        early, middle, late = early[0], middle[0], late[0]
    else:
        summed = lax.psum(partial, "rep")
        early, middle, late = summed[:PARTS], summed[PARTS : 3 * PARTS], summed[3 * PARTS :]
    (
        out_tokens,
        delta_tokens,
        delta_first,
        delta_query,
        delta_key,
        delta_value,
        delta_output,
        delta_second,
        delta_gate,
        delta_up,
        delta_down,
    ) = emit_pass(
        out_tokens, delta_tokens.reshape(group_count, width), gain_deltas, deltas, early, middle, late
    )
    return (
        out_tokens,
        delta_tokens,
        delta_first.reshape(first_gain.shape),
        delta_query,
        delta_key,
        delta_value,
        delta_output,
        delta_second.reshape(second_gain.shape),
        delta_gate.reshape(gate_weight.shape),
        delta_up.reshape(up_weight.shape),
        delta_down.reshape(down_weight.shape),
    )


def solution(mesh):
    placed = (
        P(("rep", "shard"), None),
        P(("rep", "shard"), None),
        P(("rep", "shard"), None),
        P(("rep", "shard")),
        P(("rep", "shard")),
        P(("rep", "shard"), None),
        P(("rep", "shard"), None),
        P("shard"),
        P("shard", None),
        P("shard", None),
        P("shard", None),
        P("shard", None),
        P("shard"),
        P("shard", None, None),
        P("shard", None, None),
        P("shard", None, None),
    )
    return jax.shard_map(
        local,
        mesh=mesh,
        in_specs=placed,
        out_specs=(
            P(("rep", "shard"), None),
            P(("rep", "shard"), None),
            P("shard"),
            P("shard", None),
            P("shard", None),
            P("shard", None),
            P("shard", None),
            P("shard"),
            P("shard", None, None),
            P("shard", None, None),
            P("shard", None, None),
        ),
        check_vma=False,
    )
```

profile of v0, /device:TPU:0, one launch (start us, length us, event | category | flops | bytes accessed | tf_op | source)
XLA Modules:
  0.0 385.6 jit_solution(5976468036763666454)
XLA Ops:
  0.6 83.3 %front_pass.1 = (bf16[1024,3072]{1,0:T(8,128)(2,1)}, f32[8,1024]{1,0:T(8,128)}, f32[8,8,512]{2,1,0:T(8,128)}, f32[512,128]{1,0:T(8,128)}, f32[512,128]{1,0:T(8,1...) custom-call(bf16[8,64,1024]{2,1,0:T(8,128)(2,1)} %bitcast.22, ...), custom_call_target="tpu_custom_call" | custom-call | flops 12884901888 | bytes 67108864 | tf_op jit(solution)/shard_map/front_pass/pallas_call | solution.py:1383
  84.0 95.0 %expert_pass.1 = (bf16[8,512,1024]{2,1,0:T(8,128)(2,1)}, bf16[8,512,2048]{2,1,0:T(8,128)(2,1)}, bf16[48,64,1024]{2,1,0:T(8,128)(2,1)}, bf16[8,64,1024]{2,1,0:T(8,128)(2,1)}) custom-call(bf16[512,1024]{1,0:T(8,128)(2,1)} %get-tuple-element.49.refs_0_, bf16[8,8,64,1024]{3,2,1,0:T(8,128)(2,1)} %bitcast.31, f32[8,8,512]{2,1,0:T(8,128)} %get-tuple-element.51.refs_2_, ...), custom_call_target="tpu_custom_call" | custom-call | flops 51539607552 | bytes 67108864 | tf_op jit(solution)/shard_map/expert_pass/pallas_call | solution.py:527
  179.0 70.6 %return_pass.1 = (f32[512,1024]{1,0:T(8,128)}, bf16[4,512,1024]{2,1,0:T(8,128)(2,1)}, bf16[16,64,1024]{2,1,0:T(8,128)(2,1)}) custom-call(bf16[8,512,2048]{2,1,0:T(8,128)(2,1)} %get-tuple-element.52.refs_0_, bf16[8,8,64,1024]{3,2,1,0:T(8,128)(2,1)} %bitcast.32, bf16[2,1024,512]{2,1,0:T(8,128)(2,1)} %refs_2_.1, bf16[2,1024,512]{2,1,0:T(8,128)(2,1)} %refs_3_.4, ...), custom_call_target="tpu_custom_call" | custom-call | flops 25769803776 | bytes 67108864 | tf_op jit(solution)/shard_map/return_pass/pallas_call | solution.py:882
  249.6 125.7 %finish_pass.1 = (bf16[6,64,1024]{2,1,0:T(8,128)(2,1)}, f32[8,128]{1,0:T(8,128)}, bf16[8,64,1024]{2,1,0:T(8,128)(2,1)}, bf16[512,1024]{1,0:T(8,128)(2,1)}, bf16[24,64,1024]{2,1,0:T(8,128)(2,1)}) custom-call(f32[512,1024]{1,0:T(8,128)} %get-tuple-element.56.refs_0_, bf16[8,512,1024]{2,1,0:T(8,128)(2,1)} %get-tuple-element.50.refs_1_, s32[1,512]{1,0:T(1,128)} %bitcast.26, ...), custom_call_target="tpu_custom_call" | custom-call | flops 25769803776 | bytes 16777216 | tf_op jit(solution)/shard_map/finish_pass/pallas_call | solution.py:1907
  375.3 10.1 %emit_pass.1 = (bf16[512,1024]{1,0:T(8,128)(2,1)}, bf16[512,1024]{1,0:T(8,128)(2,1)}, f32[1,128]{1,0:T(1,128)}, f32[128,1024]{1,0:T(8,128)}, f32[128,512]{1,0:T(...) custom-call(bf16[512,1024]{1,0:T(8,128)(2,1)} %get-tuple-element.69., ...), custom_call_target="tpu_custom_call" | custom-call | flops 1048576 | bytes 16777216 | tf_op jit(solution)/shard_map/emit_pass/pallas_call | solution.py:2039
where the time goes:
time: 386 us
  Pallas kernels  385 us (100%)
    pallas_call x1, Pallas kernels, finish_pass(): pl.pallas_call(functools.partial(finish_kernel, count, reps), name='finis...  126 us
    pallas_call x1, Pallas kernels, expert_pass(): pl.pallas_call(functools.partial(expert_kernel, count, reps), name='exper...  95 us
    pallas_call x1, Pallas kernels, front_pass(): pl.pallas_call(functools.partial(front_kernel, count), name='front_pass',...  83.3 us
    pallas_call x1, Pallas kernels, return_pass(): pl.pallas_call(functools.partial(return_kernel, count, reps), name='retur...  70.6 us
    pallas_call x1, Pallas kernels, emit_pass(): pl.pallas_call(emit_kernel, name='emit_pass', grid=(steps,), out_shape=(s...  10.1 us

commit v1 on v0

--- a/solution.py
+++ b/solution.py
@@ -190,17 +190,21 @@
 
         lax.fori_loop(begin, end, step, 0)
 
-    def finish(self):
+    def receive(self):
         @pl.when(self.outer)
         def _():
-            def receive(i):
+            def step(i):
                 self.copy(2, i).wait_recv()
                 if self.held is None:
                     self.out[i] = self.first[i]
                 else:
                     self.put(i).start()
 
-            self.loop(receive)
+            self.loop(step)
+
+    def finish(self):
+        @pl.when(self.outer)
+        def _():
             self.loop(lambda i: self.copy(0, i).wait_send())
 
         @pl.when(self.inner)
@@ -412,19 +416,19 @@
     if lined:
         line = Line(rep, me, stage, line_out, *refs[14:], count=PARTS)
 
-    def wrap_up(e):
-        size = acc_down.shape[1] // PARTS
-        side = acc_both.shape[1] // (2 * PARTS)
+    def spread(e, both, down):
+        size = down.shape[0] // PARTS
+        side = both.shape[0] // (2 * PARTS)
         base = e * 3 * PARTS
         for i in range(PARTS):
-            down = base + (0 if e == 0 else 2 * PARTS) + i
-            stage[down] = acc_down[e, i * size : (i + 1) * size, :].astype(low)
+            at = base + (0 if e == 0 else 2 * PARTS) + i
+            stage[at] = down[i * size : (i + 1) * size, :].astype(low)
             for which in range(2):
                 at = base + (PARTS if e == 0 else 0) + which * PARTS + i
                 for piece in range(2):
                     span = slice((2 * i + piece) * side, (2 * i + piece + 1) * side)
-                    stage[at, :, piece * hidden : (piece + 1) * hidden] = acc_both[
-                        e, span, which * hidden : (which + 1) * hidden
+                    stage[at, :, piece * hidden : (piece + 1) * hidden] = both[
+                        span, which * hidden : (which + 1) * hidden
                     ].astype(low)
         stage_copy(e).start()
 
@@ -449,7 +453,7 @@
             slope_copy(t + 1).start()
 
         if lined:
-            line.ticks(2 * (t - swap - 1), 2 * (t - swap))
+            line.tick(2 * (t - swap - 1))
         slope_copy(t).wait()
 
         @pl.when(t >= 2)
@@ -474,29 +478,35 @@
             grad_buf[slot, :, pl.ds(hidden + part * TILE, TILE)] = (dh * act).astype(low)
         hidden_copy(t).start()
         grad_copy(t).start()
-
-        def add(acc, value):
-            @pl.when(k == 0)
-            def _():
-                acc[e] = value
-
-            @pl.when(k > 0)
-            def _():
-                acc[e] += value
-
-        add(acc_both, matmul(x, grad_buf[slot], TN))
-        add(acc_down, matmul(hidden_buf[slot], dy, TN))
+        if lined:
+            line.tick(2 * (t - swap) - 1)
+
+        both = matmul(x, grad_buf[slot], TN)
+        down = matmul(hidden_buf[slot], dy, TN)
+
+        @pl.when(k == 0)
+        def _():
+            acc_both[e] = both
+            acc_down[e] = down
+
+        @pl.when((k > 0) & (k < count - 1))
+        def _():
+            acc_both[e] += both
+            acc_down[e] += down
 
         @pl.when(t == swap - 1)
         def _():
-            wrap_up(0)
+            spread(0, acc_both[0] + both, acc_down[0] + down)
             if lined:
                 line.start()
 
+        @pl.when(t == turns - 1)
+        def _():
+            spread(1, acc_both[1] + both, acc_down[1] + down)
+
         return carry
 
     lax.fori_loop(0, turns, step, 0)
-    wrap_up(1)
     if lined:
         line.ticks(2 * (turns - swap - 1), PARTS + LAG)
     for t in (turns - 2, turns - 1):
@@ -505,6 +515,7 @@
     gather.finish(())
     stage_copy(0).wait()
     if lined:
+        line.receive()
         line.finish()
     stage_copy(1).wait()
 
@@ -781,7 +792,7 @@
     if lined:
         line.start()
 
-    def sweep(base, load, part, combine, before):
+    def sweep(base, load, part, combine, pace):
         def item_step(item, carry):
             turn = item // 2
             mask = mask_of(turn)
@@ -808,7 +819,7 @@
                 combine(turn, mask)
 
             if lined:
-                line.tick(before + item - 2)
+                line.ticks(pace(item) - 2, pace(item + 1) - 2)
             return carry
 
         lax.fori_loop(0, 2 * pairs, item_step, 0)
@@ -817,11 +828,11 @@
 
     for copy in staging:
         copy.wait()
-    sweep(0, grad_load, grad_part, grad_combine, 0)
+    sweep(0, grad_load, grad_part, grad_combine, lambda item: 3 * item // 2)
     hidden_load(0).start()
-    sweep(pairs, hidden_load, hidden_part, hidden_combine, 2 * pairs)
+    sweep(pairs, hidden_load, hidden_part, hidden_combine, lambda item: 3 * pairs + item)
     if lined:
-        line.ticks(4 * pairs - 2, 2 * PARTS - 1)
+        line.ticks(5 * pairs - 2, 2 * PARTS + LAG)
     if relayed:
         for side in range(2):
             half_copy(side).wait_recv()
@@ -842,7 +853,7 @@
         for turn in (pairs - 3, pairs - 2):
             far_copy(turn, me).wait_send()
     if lined:
-        line.ticks(2 * PARTS - 1, 2 * PARTS + LAG)
+        line.receive()
     if relayed:
         for side in range(2):
             relay_copy(1, side, piece.at[0]).wait_recv()
@@ -1729,7 +1740,7 @@
         value_parts = []
         query_parts = [[], []]
         for a in range(2):
-            tick(5 + 2 * g + a, 6 + 2 * g + a)
+            tick(5 + 3 * (2 * g + a) // 2, 5 + 3 * (2 * g + a + 1) // 2)
             key_h = keys[:, a * HEAD_SIZE : (a + 1) * HEAD_SIZE]
             value_h = values[:, a * HEAD_SIZE : (a + 1) * HEAD_SIZE]
             key_slope = [None, None]
@@ -1780,23 +1791,25 @@
         copy.wait()
     loops = key_width // 128
     lax.fori_loop(0, loops, heads, 0)
-    done = 5 + 2 * loops
+    done = 5 + 3 * loops
     own_piece.start()
     inputs = input_ref[...].astype(full)
     scale = lax.rsqrt(jnp.mean(inputs * inputs, axis=1, keepdims=True) + EPS)
     normed[...] = (inputs * scale * gain_ref[0:1, :]).astype(low)
+    tick(done, done + 1)
 
     def input_part(at, carry):
+        tick(done + 1 + at // 2, done + 1 + at // 2 + at % 2)
         spot = pl.ds(pl.multiple_of(at * 512, 512), 512)
         delta[:, spot] = matmul(normed[...], backs[:, spot], TN).astype(low)
         return carry
 
     lax.fori_loop(0, joined // 512, input_part, 0)
     exchange(1)
-    tick(done, done + 1)
     slope = matmul(backs[...], weight_ref[:, :joined], NT)
+    tick(done + 3, done + 4)
     combine(1)
-    tick(done + 1, done + 2)
+    tick(done + 4, done + 5)
     scaled = slope * gain_ref[0:1, :]
     first = jnp.sum(slope * inputs * scale, axis=0, keepdims=True)
     for owner in range(count):
@@ -1804,6 +1817,7 @@
         gain_buf[owner, 2:8, :] = jnp.zeros((6, rows), full)
     for k in range(1, count):
         gain_copy(k).start()
+    tick(done + 5, done + 6)
     result = (
         steep[...]
         + scale * scaled
@@ -1814,7 +1828,7 @@
     for k in range(count - 1, 0, -1):
         slope_copy(k).start()
     slope_out[me] = arrived[me]
-    tick(done + 2, done + 5)
+    tick(done + 6, done + 7)
     own_piece.wait()
     result = mixed_slope[...].astype(full)
     for turn in range(1, pairs - 1):
@@ -1832,12 +1846,14 @@
     gain_line[rep] = total
     for k in range(1, reps):
         gain_line_copy(k).start()
-    tick(done + 5, done + 9)
+    tick(done + 7, 3 * PARTS + LAG - 1)
     collect(1, 2, 4)
     if lined:
         sums.start(2, 6)
-        tick(done + 9, 3 * PARTS + LAG)
+        tick(3 * PARTS + LAG - 1, 3 * PARTS + LAG)
+        line.receive()
         sums.ticks(0, 6 + LAG)
+        sums.receive()
         sums.finish()
     else:
 

time: 386 us -> 376 us (0.974)
  Pallas kernels: 385 us -> 372 us
    pallas_call x1, Pallas kernels: 126 us -> 121 us  [finish_pass(): pl.pallas_call(functools.partial(finish_kernel, count, reps), name='finis...]
    pallas_call x1, Pallas kernels: 70.6 us -> 65.8 us  [return_pass(): pl.pallas_call(functools.partial(return_kernel, count, reps), name='retur...]
where the time goes in v1:
time: 376 us; the launch traced here: 373 us
  Pallas kernels  372 us (99%)
    pallas_call x1, Pallas kernels, finish_pass(): pl.pallas_call(functools.partial(finish_kernel, count, reps), name='finis...  121 us
    pallas_call x1, Pallas kernels, expert_pass(): pl.pallas_call(functools.partial(expert_kernel, count, reps), name='exper...  92.5 us
    pallas_call x1, Pallas kernels, front_pass(): pl.pallas_call(functools.partial(front_kernel, count), name='front_pass',...  83.3 us
    pallas_call x1, Pallas kernels, return_pass(): pl.pallas_call(functools.partial(return_kernel, count, reps), name='retur...  65.8 us
    pallas_call x1, Pallas kernels, emit_pass(): pl.pallas_call(emit_kernel, name='emit_pass', grid=(steps,), out_shape=(s...  10.1 us

profile of v1, /device:TPU:0, one launch (start us, length us, event | category | flops | bytes accessed | tf_op | source)
XLA Modules:
  0.0 373.4 jit_solution(15239687624403633575)
XLA Ops:
  0.6 83.3 %front_pass.1 = (bf16[1024,3072]{1,0:T(8,128)(2,1)}, f32[8,1024]{1,0:T(8,128)}, f32[8,8,512]{2,1,0:T(8,128)}, f32[512,128]{1,0:T(8,128)}, f32[512,128]{1,0:T(8,1...) custom-call(bf16[8,64,1024]{2,1,0:T(8,128)(2,1)} %bitcast.22, ...), custom_call_target="tpu_custom_call" | custom-call | flops 12884901888 | bytes 67108864 | tf_op jit(solution)/shard_map/front_pass/pallas_call | solution.py:1394
  84.0 92.5 %expert_pass.1 = (bf16[8,512,1024]{2,1,0:T(8,128)(2,1)}, bf16[8,512,2048]{2,1,0:T(8,128)(2,1)}, bf16[48,64,1024]{2,1,0:T(8,128)(2,1)}, bf16[8,64,1024]{2,1,0:T(8,128)(2,1)}) custom-call(bf16[512,1024]{1,0:T(8,128)(2,1)} %get-tuple-element.49.refs_0_, bf16[8,8,64,1024]{3,2,1,0:T(8,128)(2,1)} %bitcast.31, f32[8,8,512]{2,1,0:T(8,128)} %get-tuple-element.51.refs_2_, ...), custom_call_target="tpu_custom_call" | custom-call | flops 51539607552 | bytes 67108864 | tf_op jit(solution)/shard_map/expert_pass/pallas_call | solution.py:538
  176.5 65.8 %return_pass.1 = (f32[512,1024]{1,0:T(8,128)}, bf16[4,512,1024]{2,1,0:T(8,128)(2,1)}, bf16[16,64,1024]{2,1,0:T(8,128)(2,1)}) custom-call(bf16[8,512,2048]{2,1,0:T(8,128)(2,1)} %get-tuple-element.52.refs_0_, bf16[8,8,64,1024]{3,2,1,0:T(8,128)(2,1)} %bitcast.32, bf16[2,1024,512]{2,1,0:T(8,128)(2,1)} %refs_2_.1, bf16[2,1024,512]{2,1,0:T(8,128)(2,1)} %refs_3_.4, ...), custom_call_target="tpu_custom_call" | custom-call | flops 25769803776 | bytes 67108864 | tf_op jit(solution)/shard_map/return_pass/pallas_call | solution.py:893
  242.3 120.6 %finish_pass.1 = (bf16[6,64,1024]{2,1,0:T(8,128)(2,1)}, f32[8,128]{1,0:T(8,128)}, bf16[8,64,1024]{2,1,0:T(8,128)(2,1)}, bf16[512,1024]{1,0:T(8,128)(2,1)}, bf16[24,64,1024]{2,1,0:T(8,128)(2,1)}) custom-call(f32[512,1024]{1,0:T(8,128)} %get-tuple-element.56.refs_0_, bf16[8,512,1024]{2,1,0:T(8,128)(2,1)} %get-tuple-element.50.refs_1_, s32[1,512]{1,0:T(1,128)} %bitcast.26, ...), custom_call_target="tpu_custom_call" | custom-call | flops 25769803776 | bytes 16777216 | tf_op jit(solution)/shard_map/finish_pass/pallas_call | solution.py:1923
  362.9 10.1 %emit_pass.1 = (bf16[512,1024]{1,0:T(8,128)(2,1)}, bf16[512,1024]{1,0:T(8,128)(2,1)}, f32[1,128]{1,0:T(1,128)}, f32[128,1024]{1,0:T(8,128)}, f32[128,512]{1,0:T(...) custom-call(bf16[512,1024]{1,0:T(8,128)(2,1)} %get-tuple-element.69., ...), custom_call_target="tpu_custom_call" | custom-call | flops 1048576 | bytes 16777216 | tf_op jit(solution)/shard_map/emit_pass/pallas_call | solution.py:2055

commit v2 on v1

--- a/solution.py
+++ b/solution.py
@@ -421,10 +421,10 @@
         side = both.shape[0] // (2 * PARTS)
         base = e * 3 * PARTS
         for i in range(PARTS):
-            at = base + (0 if e == 0 else 2 * PARTS) + i
+            at = base + 2 * PARTS * e + i
             stage[at] = down[i * size : (i + 1) * size, :].astype(low)
             for which in range(2):
-                at = base + (PARTS if e == 0 else 0) + which * PARTS + i
+                at = base + PARTS * (1 - e) + which * PARTS + i
                 for piece in range(2):
                     span = slice((2 * i + piece) * side, (2 * i + piece + 1) * side)
                     stage[at, :, piece * hidden : (piece + 1) * hidden] = both[
@@ -494,15 +494,15 @@
             acc_both[e] += both
             acc_down[e] += down
 
-        @pl.when(t == swap - 1)
+        @pl.when((t == swap - 1) | (t == turns - 1))
         def _():
-            spread(0, acc_both[0] + both, acc_down[0] + down)
-            if lined:
+            spread(e, acc_both[e] + both, acc_down[e] + down)
+
+        if lined:
+
+            @pl.when(t == swap - 1)
+            def _():
                 line.start()
-
-        @pl.when(t == turns - 1)
-        def _():
-            spread(1, acc_both[1] + both, acc_down[1] + down)
 
         return carry
 

time: 376 us -> 374 us (level)
  no operation moved by 1% of the time
where the time goes in v2:
time: 374 us; the launch traced here: 373 us
  Pallas kernels  372 us (99%)
    pallas_call x1, Pallas kernels, finish_pass(): pl.pallas_call(functools.partial(finish_kernel, count, reps), name='finis...  121 us
    pallas_call x1, Pallas kernels, expert_pass(): pl.pallas_call(functools.partial(expert_kernel, count, reps), name='exper...  92.5 us
    pallas_call x1, Pallas kernels, front_pass(): pl.pallas_call(functools.partial(front_kernel, count), name='front_pass',...  83.3 us
    pallas_call x1, Pallas kernels, return_pass(): pl.pallas_call(functools.partial(return_kernel, count, reps), name='retur...  65.8 us
    pallas_call x1, Pallas kernels, emit_pass(): pl.pallas_call(emit_kernel, name='emit_pass', grid=(steps,), out_shape=(s...  10.1 us

profile of v2, /device:TPU:0, one launch (start us, length us, event | category | flops | bytes accessed | tf_op | source)
XLA Modules:
  0.0 373.1 jit_solution(15373656168658308215)
XLA Ops:
  0.6 83.3 %front_pass.1 = (bf16[1024,3072]{1,0:T(8,128)(2,1)}, f32[8,1024]{1,0:T(8,128)}, f32[8,8,512]{2,1,0:T(8,128)}, f32[512,128]{1,0:T(8,128)}, f32[512,128]{1,0:T(8,1...) custom-call(bf16[8,64,1024]{2,1,0:T(8,128)(2,1)} %bitcast.22, ...), custom_call_target="tpu_custom_call" | custom-call | flops 12884901888 | bytes 67108864 | tf_op jit(solution)/shard_map/front_pass/pallas_call | solution.py:1394
  84.0 92.5 %expert_pass.1 = (bf16[8,512,1024]{2,1,0:T(8,128)(2,1)}, bf16[8,512,2048]{2,1,0:T(8,128)(2,1)}, bf16[48,64,1024]{2,1,0:T(8,128)(2,1)}, bf16[8,64,1024]{2,1,0:T(8,128)(2,1)}) custom-call(bf16[512,1024]{1,0:T(8,128)(2,1)} %get-tuple-element.49.refs_0_, bf16[8,8,64,1024]{3,2,1,0:T(8,128)(2,1)} %bitcast.31, f32[8,8,512]{2,1,0:T(8,128)} %get-tuple-element.51.refs_2_, ...), custom_call_target="tpu_custom_call" | custom-call | flops 51539607552 | bytes 67108864 | tf_op jit(solution)/shard_map/expert_pass/pallas_call | solution.py:538
  176.5 65.8 %return_pass.1 = (f32[512,1024]{1,0:T(8,128)}, bf16[4,512,1024]{2,1,0:T(8,128)(2,1)}, bf16[16,64,1024]{2,1,0:T(8,128)(2,1)}) custom-call(bf16[8,512,2048]{2,1,0:T(8,128)(2,1)} %get-tuple-element.52.refs_0_, bf16[8,8,64,1024]{3,2,1,0:T(8,128)(2,1)} %bitcast.32, bf16[2,1024,512]{2,1,0:T(8,128)(2,1)} %refs_2_.1, bf16[2,1024,512]{2,1,0:T(8,128)(2,1)} %refs_3_.4, ...), custom_call_target="tpu_custom_call" | custom-call | flops 25769803776 | bytes 67108864 | tf_op jit(solution)/shard_map/return_pass/pallas_call | solution.py:893
  242.3 120.5 %finish_pass.1 = (bf16[6,64,1024]{2,1,0:T(8,128)(2,1)}, f32[8,128]{1,0:T(8,128)}, bf16[8,64,1024]{2,1,0:T(8,128)(2,1)}, bf16[512,1024]{1,0:T(8,128)(2,1)}, bf16[24,64,1024]{2,1,0:T(8,128)(2,1)}) custom-call(f32[512,1024]{1,0:T(8,128)} %get-tuple-element.56.refs_0_, bf16[8,512,1024]{2,1,0:T(8,128)(2,1)} %get-tuple-element.50.refs_1_, s32[1,512]{1,0:T(1,128)} %bitcast.26, ...), custom_call_target="tpu_custom_call" | custom-call | flops 25769803776 | bytes 16777216 | tf_op jit(solution)/shard_map/finish_pass/pallas_call | solution.py:1923
  362.8 10.1 %emit_pass.1 = (bf16[512,1024]{1,0:T(8,128)(2,1)}, bf16[512,1024]{1,0:T(8,128)(2,1)}, f32[1,128]{1,0:T(1,128)}, f32[128,1024]{1,0:T(8,128)}, f32[128,512]{1,0:T(...) custom-call(bf16[512,1024]{1,0:T(8,128)(2,1)} %get-tuple-element.69., ...), custom_call_target="tpu_custom_call" | custom-call | flops 1048576 | bytes 16777216 | tf_op jit(solution)/shard_map/emit_pass/pallas_call | solution.py:2055

commit v3 on v2

--- a/solution.py
+++ b/solution.py
@@ -2040,7 +2040,7 @@
     rows = gains.shape[1]
     _, high, wide = early.shape
     hidden = high * PARTS
-    steps = 4
+    steps = 2
     each = PARTS // steps
 
     def moving(*block):

time: 374 us -> 372 us (level)
  no operation moved by 1% of the time
where the time goes in v3:
time: 372 us
  Pallas kernels  371 us (100%)
    pallas_call x1, Pallas kernels, finish_pass(): pl.pallas_call(functools.partial(finish_kernel, count, reps), name='finis...  121 us
    pallas_call x1, Pallas kernels, expert_pass(): pl.pallas_call(functools.partial(expert_kernel, count, reps), name='exper...  92.5 us
    pallas_call x1, Pallas kernels, front_pass(): pl.pallas_call(functools.partial(front_kernel, count), name='front_pass',...  83.3 us
    pallas_call x1, Pallas kernels, return_pass(): pl.pallas_call(functools.partial(return_kernel, count, reps), name='retur...  65.8 us
    pallas_call x1, Pallas kernels, emit_pass(): pl.pallas_call(emit_kernel, name='emit_pass', grid=(steps,), out_shape=(s...  8.77 us

profile of v3, /device:TPU:0, one launch (start us, length us, event | category | flops | bytes accessed | tf_op | source)
XLA Modules:
  0.0 371.8 jit_solution(5593447836744581120)
XLA Ops:
  0.6 83.3 %front_pass.1 = (bf16[1024,3072]{1,0:T(8,128)(2,1)}, f32[8,1024]{1,0:T(8,128)}, f32[8,8,512]{2,1,0:T(8,128)}, f32[512,128]{1,0:T(8,128)}, f32[512,128]{1,0:T(8,1...) custom-call(bf16[8,64,1024]{2,1,0:T(8,128)(2,1)} %bitcast.22, ...), custom_call_target="tpu_custom_call" | custom-call | flops 12884901888 | bytes 67108864 | tf_op jit(solution)/shard_map/front_pass/pallas_call | solution.py:1394
  84.0 92.5 %expert_pass.1 = (bf16[8,512,1024]{2,1,0:T(8,128)(2,1)}, bf16[8,512,2048]{2,1,0:T(8,128)(2,1)}, bf16[48,64,1024]{2,1,0:T(8,128)(2,1)}, bf16[8,64,1024]{2,1,0:T(8,128)(2,1)}) custom-call(bf16[512,1024]{1,0:T(8,128)(2,1)} %get-tuple-element.49.refs_0_, bf16[8,8,64,1024]{3,2,1,0:T(8,128)(2,1)} %bitcast.31, f32[8,8,512]{2,1,0:T(8,128)} %get-tuple-element.51.refs_2_, ...), custom_call_target="tpu_custom_call" | custom-call | flops 51539607552 | bytes 67108864 | tf_op jit(solution)/shard_map/expert_pass/pallas_call | solution.py:538
  176.5 65.8 %return_pass.1 = (f32[512,1024]{1,0:T(8,128)}, bf16[4,512,1024]{2,1,0:T(8,128)(2,1)}, bf16[16,64,1024]{2,1,0:T(8,128)(2,1)}) custom-call(bf16[8,512,2048]{2,1,0:T(8,128)(2,1)} %get-tuple-element.52.refs_0_, bf16[8,8,64,1024]{3,2,1,0:T(8,128)(2,1)} %bitcast.32, bf16[2,1024,512]{2,1,0:T(8,128)(2,1)} %refs_2_.1, bf16[2,1024,512]{2,1,0:T(8,128)(2,1)} %refs_3_.4, ...), custom_call_target="tpu_custom_call" | custom-call | flops 25769803776 | bytes 67108864 | tf_op jit(solution)/shard_map/return_pass/pallas_call | solution.py:893
  242.3 120.5 %finish_pass.1 = (bf16[6,64,1024]{2,1,0:T(8,128)(2,1)}, f32[8,128]{1,0:T(8,128)}, bf16[8,64,1024]{2,1,0:T(8,128)(2,1)}, bf16[512,1024]{1,0:T(8,128)(2,1)}, bf16[24,64,1024]{2,1,0:T(8,128)(2,1)}) custom-call(f32[512,1024]{1,0:T(8,128)} %get-tuple-element.56.refs_0_, bf16[8,512,1024]{2,1,0:T(8,128)(2,1)} %get-tuple-element.50.refs_1_, s32[1,512]{1,0:T(1,128)} %bitcast.26, ...), custom_call_target="tpu_custom_call" | custom-call | flops 25769803776 | bytes 16777216 | tf_op jit(solution)/shard_map/finish_pass/pallas_call | solution.py:1923
  362.8 8.8 %emit_pass.1 = (bf16[512,1024]{1,0:T(8,128)(2,1)}, bf16[512,1024]{1,0:T(8,128)(2,1)}, f32[1,128]{1,0:T(1,128)}, f32[128,1024]{1,0:T(8,128)}, f32[128,512]{1,0:T(...) custom-call(bf16[512,1024]{1,0:T(8,128)(2,1)} %get-tuple-element.69., ...), custom_call_target="tpu_custom_call" | custom-call | flops 1048576 | bytes 16777216 | tf_op jit(solution)/shard_map/emit_pass/pallas_call | solution.py:2055
